TPU v7x, 32 devices: a whole 2x2x4 slice. The times are simulated.
32 devices in a mesh: group: 2 (over y), ctx: 8 (over z, core), head: 2 (over x).
Axes of the slice: x: 2, y: 2, z: 4, core: 2. Of those that a mesh axis runs over, the one named last changes fastest.
Arguments:
- queries: bfloat16 [2048, 4096], P(('group', 'ctx'), 'head'), parts along dimension 0, may hold values from -6 to 6
- keys: bfloat16 [2048, 512], P(('group', 'ctx'), 'head'), parts along dimension 0, may hold values from -6 to 6
- values: bfloat16 [2048, 512], P(('group', 'ctx'), 'head'), parts along dimension 0, may hold values from -6 to 6
- sinks: float32 [64], P('head'), may hold values from 0 to 4
- segments: int32 [2048], P('group'), parts along dimension 0, may hold values from 0 to 3, never falling along the last dimension, each value on 1 to 768 neighbouring positions
- hidden_in: bfloat16 [2048, 2880], P(('group', 'ctx')), parts along dimension 0, may hold values from -6 to 6
- routes: int32 [2048, 4], P(('group', 'ctx')), parts along dimension 0, may hold values from 0 to 7, all different within a row; in each aligned block of 64 rows (0 to 63, 64 to 127, ...) at most 48 rows name the same one
- w_out: bfloat16 [4096, 2880], P('head'), may hold values from -0.09375 to 0.09375
- norm_gain: float32 [2880], replicated, may hold values from 0.1 to 1.9
- router: bfloat16 [2880, 8], replicated, may hold values from -0.109375 to 0.109375
- w_gate_up: bfloat16 [8, 2, 2880, 2880], P('ctx', None, None, 'head'), may hold values from -0.109375 to 0.109375
- w_down: bfloat16 [8, 2880, 2880], P('ctx', 'head'), may hold values from -0.109375 to 0.109375
Outputs:
- layer_out: bfloat16 [2048, 2880], P(('group', 'ctx', 'head')), parts along dimension 0
There are 2 independent parts, one for each index of `group`. A program takes and returns all parts, laid end to end along the dimension named above; an argument that names none is the same for every part. Nothing has to cross between parts.
Inputs may be any that keep to these rules, and one draw needn't show every extreme that they name: `routes`: each row names 4 different experts; in each aligned block of 64 rows no expert is named by more than 48 rows, a bound that some block reaches. `segments`: requests fill consecutive positions in order; the longest has 768 positions.
All inputs are finite; a program needn't handle non-finite values.
Results may differ from a plain program's by a relative error of at most 0.015.
Values may be sent and summed in bfloat16 or wider, within the bound.
A program may use at most 128 MiB of HBM per device.

v0:
```python
import jax
import jax.numpy as jnp
from jax import lax
from jax.sharding import PartitionSpec as P

HEAD_SIZE = 64


masked_value = -1e30


def fold_step(state_in, pieces, query_grid, tok_pos, tok_seg, segments):
    running_max, running_sum, weighted = state_in
    key_piece, value_piece = pieces
    row_count = key_piece.shape[0]
    kv_groups = query_grid.shape[1]
    key_grid = key_piece.reshape(row_count, kv_groups, -1)
    value_grid = value_piece.reshape(row_count, kv_groups, -1)
    scores = jnp.einsum(
        "tcgd,ncd->cgtn", query_grid, key_grid, preferred_element_type=jnp.float32
    ) * HEAD_SIZE ** (-0.5)
    key_pos = jnp.arange(row_count, dtype=jnp.int32)
    visible = (key_pos[None, :] <= tok_pos[:, None]) & (segments[None, :] == tok_seg[:, None])
    scores = jnp.where(visible, scores, masked_value)
    new_max = jnp.maximum(running_max, jnp.max(scores, axis=-1))
    weights = jnp.where(visible, jnp.exp(scores - new_max[..., None]), 0.0)
    rescale = jnp.exp(running_max - new_max)
    running_sum = running_sum * rescale + jnp.sum(weights, axis=-1)
    weighted = weighted * rescale[..., None] + jnp.einsum(
        "cgtn,ncd->cgtd",
        weights.astype(jnp.bfloat16),
        value_grid,
        preferred_element_type=jnp.float32,
    )
    return (new_max, running_sum, weighted)


def rms_norm(residual, norm_gain):
    widened = residual.astype(jnp.float32)
    scale_rows = lax.rsqrt(jnp.mean(widened * widened, axis=-1, keepdims=True) + 1e-05)
    return (widened * scale_rows * norm_gain).astype(jnp.bfloat16)


def gate_weights(normed, router, route_ids):
    logits = jnp.dot(normed, router, preferred_element_type=jnp.float32)
    onehot = (
        route_ids[:, :, None] == jnp.arange(router.shape[1], dtype=jnp.int32)[None, None, :]
    ).astype(jnp.float32)
    picked = jnp.sum(onehot * logits[:, None, :], axis=-1)
    return jax.nn.softmax(picked, axis=-1)


def slot_index(route_ids, experts, capacity):
    flat_ids = route_ids.reshape(-1)
    onehot = (flat_ids[:, None] == jnp.arange(experts, dtype=jnp.int32)[None, :]).astype(jnp.int32)
    before = jnp.cumsum(onehot, axis=0) - onehot
    position = jnp.sum(before * onehot, axis=1)
    return (flat_ids * capacity + position).reshape(route_ids.shape)


def placer_matrix(slot_ids, slot_count):
    match = slot_ids[None, :, :] == jnp.arange(slot_count, dtype=jnp.int32)[:, None, None]
    return jnp.sum(match.astype(jnp.float32), axis=-1).astype(jnp.bfloat16)


def expert_piece(token_rows, w_gate_up, w_down):
    gate_pre = jnp.dot(token_rows, w_gate_up[0, 0], preferred_element_type=jnp.float32)
    up_pre = jnp.dot(token_rows, w_gate_up[0, 1], preferred_element_type=jnp.float32)
    activation = (gate_pre * jax.nn.sigmoid(1.702 * gate_pre) * (up_pre + 1.0)).astype(jnp.bfloat16)
    return jnp.dot(activation, w_down[0], preferred_element_type=jnp.float32).astype(jnp.bfloat16)


def body(
    queries,
    keys,
    values,
    sinks,
    segments,
    hidden_in,
    routes,
    w_out,
    norm_gain,
    router,
    w_gate_up,
    w_down,
):
    n_ctx = lax.axis_size("ctx")
    n_head = lax.axis_size("head")
    tok_count = queries.shape[0]
    top_count = routes.shape[1]
    kv_groups = keys.shape[1] // HEAD_SIZE
    group_share = queries.shape[1] // (kv_groups * HEAD_SIZE)
    q_start = lax.axis_index("ctx") * tok_count
    tok_pos = q_start + jnp.arange(tok_count, dtype=jnp.int32)
    tok_seg = lax.dynamic_slice_in_dim(segments, q_start, tok_count, 0)
    query_grid = queries.reshape(tok_count, kv_groups, group_share, HEAD_SIZE)
    sink_grid = sinks.reshape(kv_groups, group_share, 1) * jnp.ones((1, 1, tok_count), jnp.float32)
    initial = (
        sink_grid,
        jnp.ones_like(sink_grid),
        jnp.zeros((kv_groups, group_share, tok_count, HEAD_SIZE), jnp.float32),
    )
    running_max, running_sum, weighted = fold_step(
        initial,
        (
            lax.all_gather(keys, "ctx", axis=0, tiled=True),
            lax.all_gather(values, "ctx", axis=0, tiled=True),
        ),
        query_grid,
        tok_pos,
        tok_seg,
        segments,
    )
    attended = (
        (weighted / running_sum[..., None])
        .transpose(2, 0, 1, 3)
        .reshape(tok_count, -1)
        .astype(jnp.bfloat16)
    )
    own_rows = tok_count // n_head
    row_start = lax.axis_index("head") * own_rows
    capacity = max(2, min(tok_count // n_head, 3 * tok_count * top_count // (2 * n_head * n_ctx)))
    head_sums = lax.psum_scatter(
        jnp.dot(attended, w_out, preferred_element_type=jnp.float32).astype(jnp.bfloat16),
        "head",
        scatter_dimension=0,
        tiled=True,
    ).astype(jnp.float32)
    own_hidden = lax.dynamic_slice_in_dim(hidden_in, row_start, own_rows, 0)
    residual = (own_hidden.astype(jnp.float32) + head_sums).astype(jnp.bfloat16)
    normed = rms_norm(residual, norm_gain)
    own_routes = lax.dynamic_slice_in_dim(routes, row_start, own_rows, 0)
    gates = gate_weights(normed, router, own_routes)
    slot_ids = slot_index(own_routes, n_ctx, capacity)
    placer = placer_matrix(slot_ids, n_ctx * capacity)
    outgoing = jnp.dot(placer, normed, preferred_element_type=jnp.float32).astype(jnp.bfloat16)
    arrived = lax.all_to_all(outgoing, "ctx", split_axis=0, concat_axis=0, tiled=True)
    pieces = expert_piece(
        lax.all_gather(arrived, "head", axis=0, tiled=True), w_gate_up, w_down
    ).astype(jnp.float32)
    summed = lax.psum_scatter(pieces.astype(jnp.bfloat16), "head", scatter_dimension=0, tiled=True)
    returned = lax.all_to_all(summed, "ctx", split_axis=0, concat_axis=0, tiled=True)
    match = (
        slot_ids[:, :, None] == jnp.arange(n_ctx * capacity, dtype=jnp.int32)[None, None, :]
    ).astype(jnp.float32)
    combiner = jnp.sum(gates[:, :, None] * match, axis=1)
    expert_mix = jnp.dot(combiner, returned.astype(jnp.float32), precision=lax.Precision.HIGHEST)
    return (residual.astype(jnp.float32) + expert_mix).astype(jnp.bfloat16)


def solution(mesh):
    placed = (
        P(("group", "ctx"), "head"),
        P(("group", "ctx"), "head"),
        P(("group", "ctx"), "head"),
        P("head"),
        P("group"),
        P(("group", "ctx"), None),
        P(("group", "ctx"), None),
        P("head", None),
        P(),
        P(),
        P("ctx", None, None, "head"),
        P("ctx", "head", None),
    )
    return jax.shard_map(
        body,
        mesh=mesh,
        in_specs=placed,
        out_specs=P(("group", "ctx", "head"), None),
        check_vma=False,
    )
```

profile of v0, /device:TPU:0, one launch (start us, length us, event | category | flops | bytes accessed | tf_op | source)
XLA Modules:
  0.0 375.8 jit_solution(13164324825547892621)
XLA Ops:
  6.5 16.8 %all_gather.9 = bf16[1024,256]{1,0:T(8,128)(2,1)S(1)} all-gather(bf16[128,256]{1,0:T(8,128)(2,1)} %param.13), channel_id=1, replica_groups=mesh['group'=2,'ctx'=8,'head'=2] {'ctx'}, dimensions={0}, use_global_device_ids=true | all-gather | bytes 589824 | tf_op jit(solution)/shard_map/all_gather | solution.py:106
  23.4 0.2 copy.52
  23.6 1.3 copy.53
  24.9 0.7 mul.88
  25.6 0.8 dynamic_slice.10
  26.4 0.9 fusion.33
  27.3 2.4 fusion
  29.8 4.3 %fusion.1 = f32[4,8,128]{2,1,0:T(8,128)S(1)} fusion(f32[4,1024,128,8]{2,1,3,0:T(8,128)S(1)} %get-tuple-element.10, f32[4,8,128]{2,1,0:T(8,128)S(1)} %broadcast_maximum_fusion, pred[128,1024]{0,1:T(8,128)(4,1)S(1)} %fusion.33), kind=kLoop, calls=%fused_computation.3 | loop fusion | flops 20967424 | bytes 16941056 | tf_op jit(solution)/shard_map/reduce_sum | solution.py:28
  34.1 1.3 copy-done.2
  35.5 14.8 %all_gather.10 = bf16[1024,256]{1,0:T(8,128)(2,1)S(1)} all-gather(bf16[128,256]{1,0:T(8,128)(2,1)S(1)} %copy-done.3), channel_id=1, replica_groups=mesh['group'=2,'ctx'=8,'head'=2] {'ctx'}, dimensions={0}, use_global_device_ids=true | all-gather | bytes 589824 | tf_op jit(solution)/shard_map/all_gather | solution.py:107
  50.3 0.2 copy.54
  50.5 7.8 %divide_convert_fusion = bf16[128,4,8,64]{0,3,2,1:T(8,128)(2,1)S(1)} fusion(bf16[1024,4,64,1]{0,2,3,1:T(8,128)(2,1)S(1)} %bitcast.85, f32[4,1024,128,8]{2,1,3,0:T(8,128)} %copy-done.2, f32[4,8,128]{2,1,0:T(8,128)S(1)} %broadcast_maximum_fusion, pred[128,1024]{0,1:T(8,128)(4,1)S(1)} %fusion.33, f32[128,4,8]{0,2,1:T(8,128)S(1)} %get-tuple-element.8, ...), kind=kOutput, calls=%fused_computation.25 | convolution fusion | flops 558628864 | bytes 18006016 | tf_op jit(solution)/shard_map/cgtn,ncd->cgtd/dot_general | solution.py:29
  58.4 9.4 %convolution_convert_fusion.1 = bf16[128,2880]{1,0:T(8,128)(2,1)} fusion(bf16[128,2048]{0,1:T(8,128)(2,1)S(1)} %bitcast.84, bf16[2048,2880]{0,1:T(8,128)(2,1)} %param.19), kind=kOutput, calls=%fused_computation.18 | convolution fusion | flops 1510318080 | bytes 13058048 | tf_op jit(solution)/shard_map/dot_general | solution.py:124
  67.8 0.2 all-gather.2.cloned.1.call-start
  68.5 0.3 constant_dynamic-slice_fusion.1
  68.8 0.3 copy.66
  69.1 0.6 reduce-window.6
  69.7 0.2 slice_reduce_fusion
  70.4 16.1 %reduce-scatter.5.cloned.1.call-done = bf16[64,2880]{1,0:T(8,128)(2,1)} async-done(((bf16[128,2880]{1,0:T(8,128)(2,1)}), bf16[64,2880]{1,0:T(8,128)(2,1)}) %reduce-scatter.5.cloned.1.call-update) | async-done | bytes 368656 | tf_op jit(solution)/shard_map/reduce_scatter | solution.py:123
  86.5 1.2 fusion.30
  87.8 2.3 convolution_convert_fusion
  90.0 2.9 copy.59
  93.0 57.0 %all_to_all.24 = bf16[8,48,2880]{2,1,0:T(8,128)(2,1)} all-to-all(bf16[8,48,2880]{2,1,0:T(8,128)(2,1)S(1)} %bitcast.80), channel_id=1, replica_groups=mesh['group'=2,'ctx'=8,'head'=2] {'ctx'}, dimensions={0} | all-to-all | bytes 4423680 | tf_op jit(solution)/shard_map/all_to_all | solution.py:137
  150.1 58.5 %all-gather.2.cloned.1.call-done = bf16[768,2880]{1,0:T(8,128)(2,1)} async-done(((bf16[384,2880]{1,0:T(8,128)(2,1)}), bf16[768,2880]{1,0:T(8,128)(2,1)}) %all-gather.2.cloned.1.call-update) | async-done | bytes 4423696 | tf_op jit(solution)/shard_map/all_gather | solution.py:139
  208.6 12.3 %fusion.5 = f32[768,1440]{0,1:T(8,128)} fusion(bf16[768,2880]{1,0:T(8,128)(2,1)} %all-gather.2.cloned.1.call-done, bf16[1,2,2880,1440]{2,3,1,0:T(8,128)(2,1)} %param.22), kind=kOutput, calls=%fused_computation.7 | convolution fusion | flops 6370099200 | bytes 17424384 | tf_op jit(solution)/shard_map/dot_general | solution.py:68
  220.8 24.7 %fusion.14 = bf16[768,2880]{0,1:T(8,128)(2,1)} fusion(bf16[1,1440,2880]{2,1,0:T(8,128)(2,1)} %param.23, f32[768,1440]{0,1:T(8,128)} %fusion.5, bf16[768,2880]{1,0:T(8,128)(2,1)} %all-gather.2.cloned.1.call-done, bf16[1,2,2880,1440]{2,3,1,0:T(8,128)(2,1)} %param.22), kind=kOutput, calls=%fused_computation.15 | convolution fusion | flops 12751257600 | bytes 30326784 | tf_op jit(solution)/shard_map/dot_general | solution.py:70
  245.6 6.6 %copy.64 = bf16[768,2880]{1,0:T(8,128)(2,1)} copy(bf16[768,2880]{0,1:T(8,128)(2,1)} %fusion.14) | data formatting | bytes 8847360
  252.2 58.1 %reduce-scatter.7.cloned.1.call-done = bf16[384,2880]{1,0:T(8,128)(2,1)} async-done(((bf16[768,2880]{1,0:T(8,128)(2,1)}), bf16[384,2880]{1,0:T(8,128)(2,1)}) %reduce-scatter.7.cloned.1.call-update) | async-done | bytes 2211856 | tf_op jit(solution)/shard_map/reduce_scatter | solution.py:141
  310.3 4.6 %all-to-all-start.1 = ((bf16[8,48,2880]{2,1,0:T(8,128)(2,1)}), bf16[8,48,2880]{2,1,0:T(8,128)(2,1)S(1)}, u32[]{:S(2)}, u32[]{:S(2)}) async-start(bf16[8,48,2880]{2,1,0:T(8,128)(2,1)} %bitcast.81), calls=%async_computation.2 | async-start | bytes 4521984 | tf_op jit(solution)/shard_map/all_to_all | solution.py:142
  314.9 0.3 fusion.35
  315.4 52.0 %all-to-all-done.1 = bf16[8,48,2880]{2,1,0:T(8,128)(2,1)S(1)} async-done(((bf16[8,48,2880]{2,1,0:T(8,128)(2,1)}), bf16[8,48,2880]{2,1,0:T(8,128)(2,1)S(1)}, u32[]{:S(2)}, u32[]{:S(2)}) %all-to-all-start.1) | async-done | bytes 2211872 | tf_op jit(solution)/shard_map/all_to_all | solution.py:142
  367.4 1.8 fusion.19
  (39 shorter events, 1.4 us)
Async XLA Ops:
  6.5 61.9 %copy-start = (bf16[128,2880]{0,1:T(8,128)(2,1)S(1)}, bf16[128,2880]{0,1:T(8,128)(2,1)}, u32[]{:S(2)}) copy-start(bf16[128,2880]{0,1:T(8,128)(2,1)} %param.17) | copy-start | bytes 2211844
  6.5 80.0 %reduce-scatter.5.cloned.1.call-start = ((), (), s32[]{:S(2)}) async-start(), calls=%async_computation.4 | async-start | bytes 1130496 | tf_op jit(solution)/shard_map/reduce_scatter | solution.py:123
  29.7 5.7 %copy-start.2 = (f32[4,1024,128,8]{2,1,3,0:T(8,128)}, f32[4,1024,128,8]{2,1,3,0:T(8,128)S(1)}, u32[]{:S(2)}) copy-start(f32[4,1024,128,8]{2,1,3,0:T(8,128)S(1)} %get-tuple-element.10) | copy-start | bytes 50331652
  29.8 5.7 %copy-start.3 = (bf16[128,256]{1,0:T(8,128)(2,1)S(1)}, bf16[128,256]{1,0:T(8,128)(2,1)}, u32[]{:S(2)}) copy-start(bf16[128,256]{1,0:T(8,128)(2,1)} %param.14) | copy-start | bytes 196612
  58.4 9.7 %copy-start.5 = (s32[128,4]{0,1:T(4,128)S(1)}, s32[128,4]{0,1:T(4,128)}, u32[]{:S(2)}) copy-start(s32[128,4]{0,1:T(4,128)} %param.18) | copy-start | bytes 6148
  58.4 29.4 %copy-start.4 = (f32[2880]{0:T(1024)S(1)}, f32[2880]{0:T(1024)}, u32[]{:S(2)}) copy-start(f32[2880]{0:T(1024)} %param.20) | copy-start | bytes 34564
  67.8 140.7 %all-gather.2.cloned.1.call-start = ((), (), s32[]{:S(2)}) async-start(), calls=%async_computation.5 | async-start | bytes 6782976 | tf_op jit(solution)/shard_map/all_gather | solution.py:139
  150.0 160.2 %reduce-scatter.7.cloned.1.call-start = ((), (), s32[]{:S(2)}) async-start(), calls=%async_computation.6 | async-start | bytes 6782976 | tf_op jit(solution)/shard_map/reduce_scatter | solution.py:141
  245.6 69.3 %copy-start.6 = (bf16[2880,8]{0,1:T(8,128)(2,1)S(1)}, bf16[2880,8]{0,1:T(8,128)(2,1)}, u32[]{:S(2)}) copy-start(bf16[2880,8]{0,1:T(8,128)(2,1)} %param.21) | copy-start | bytes 138244
  245.6 123.7 %copy-start.1 = (bf16[128,2880]{0,1:T(8,128)(2,1)S(1)}, bf16[128,2880]{0,1:T(8,128)(2,1)}, u32[]{:S(2)}) copy-start(bf16[128,2880]{0,1:T(8,128)(2,1)} %param.17) | copy-start | bytes 2211844
  310.3 57.2 %all-to-all-start.1 = ((bf16[8,48,2880]{2,1,0:T(8,128)(2,1)}), bf16[8,48,2880]{2,1,0:T(8,128)(2,1)S(1)}, u32[]{:S(2)}, u32[]{:S(2)}) async-start(bf16[8,48,2880]{2,1,0:T(8,128)(2,1)} %bitcast.81), calls=%async_computation.2 | async-start | bytes 4521984 | tf_op jit(solution)/shard_map/all_to_all | solution.py:142
Sparse Core Ops, SparseCore 0:
  68.0 18.5 reduce-scatter.4
  150.2 58.3 all-gather.1
  252.3 57.9 reduce-scatter.6
where the time goes:
time: 376 us
  waiting for transfers between devices  185 us (49%)
  blocking collectives  88.7 us (24%)
  matrix products  61 us (16%)
  local copies, waits for them, and re-layouts  15.4 us (4%)
  between operations  13.3 us (4%)
  other arithmetic  7.75 us (2%)
  starting transfers between devices  4.87 us (1%)
    all_gather x1, waiting for transfers between devices, body(): lax.all_gather(arrived, 'head', axis=0, tiled=True)  58.5 us
    reduce_scatter x1, waiting for transfers between devices, body(): lax.psum_scatter(pieces.astype(jnp.bfloat16), 'head', scatter_dimension=0...  58.1 us
    all_to_all x1, blocking collectives, body(): lax.all_to_all(outgoing, 'ctx', split_axis=0, concat_axis=0, tiled=True)  57 us
    all_to_all x1, waiting for transfers between devices, body(): lax.all_to_all(summed, 'ctx', split_axis=0, concat_axis=0, tiled=True)  52 us
    dot_general x1, matrix products, expert_piece(): jnp.dot(activation, w_down[0], preferred_element_type=jnp.float32)  24.7 us
    all_gather x1, blocking collectives, body(): lax.all_gather(keys, 'ctx', axis=0, tiled=True)  16.8 us
    reduce_scatter x1, waiting for transfers between devices, body(): lax.psum_scatter(jnp.dot(attended, w_out, preferred_element_type=jnp.floa...  16.1 us
    all_gather x1, blocking collectives, body(): lax.all_gather(values, 'ctx', axis=0, tiled=True)  14.8 us
  transfers between devices with their start and end apart: 4, of which 4 were waited for; matrix products, arithmetic and copies ran while one was open for 1% of the time, Pallas kernels for 0%

commit v1 on v0

--- a/solution.py
+++ b/solution.py
@@ -41,33 +41,20 @@
     return (widened * scale_rows * norm_gain).astype(jnp.bfloat16)
 
 
-def gate_weights(normed, router, route_ids):
-    logits = jnp.dot(normed, router, preferred_element_type=jnp.float32)
+def expert_gates(normed_rows, router, route_rows, expert):
+    logits = jnp.dot(normed_rows, router, preferred_element_type=jnp.float32)
     onehot = (
-        route_ids[:, :, None] == jnp.arange(router.shape[1], dtype=jnp.int32)[None, None, :]
+        route_rows[:, :, None] == jnp.arange(router.shape[1], dtype=jnp.int32)[None, None, :]
     ).astype(jnp.float32)
     picked = jnp.sum(onehot * logits[:, None, :], axis=-1)
-    return jax.nn.softmax(picked, axis=-1)
+    gates = jax.nn.softmax(picked, axis=-1)
+    return jnp.sum(jnp.where(route_rows == expert, gates, 0.0), axis=1)
 
 
-def slot_index(route_ids, experts, capacity):
-    flat_ids = route_ids.reshape(-1)
-    onehot = (flat_ids[:, None] == jnp.arange(experts, dtype=jnp.int32)[None, :]).astype(jnp.int32)
-    before = jnp.cumsum(onehot, axis=0) - onehot
-    position = jnp.sum(before * onehot, axis=1)
-    return (flat_ids * capacity + position).reshape(route_ids.shape)
-
-
-def placer_matrix(slot_ids, slot_count):
-    match = slot_ids[None, :, :] == jnp.arange(slot_count, dtype=jnp.int32)[:, None, None]
-    return jnp.sum(match.astype(jnp.float32), axis=-1).astype(jnp.bfloat16)
-
-
-def expert_piece(token_rows, w_gate_up, w_down):
+def expert_activation(token_rows, w_gate_up):
     gate_pre = jnp.dot(token_rows, w_gate_up[0, 0], preferred_element_type=jnp.float32)
     up_pre = jnp.dot(token_rows, w_gate_up[0, 1], preferred_element_type=jnp.float32)
-    activation = (gate_pre * jax.nn.sigmoid(1.702 * gate_pre) * (up_pre + 1.0)).astype(jnp.bfloat16)
-    return jnp.dot(activation, w_down[0], preferred_element_type=jnp.float32).astype(jnp.bfloat16)
+    return (gate_pre * jax.nn.sigmoid(1.702 * gate_pre) * (up_pre + 1.0)).astype(jnp.bfloat16)
 
 
 def body(
@@ -100,12 +87,15 @@
         jnp.ones_like(sink_grid),
         jnp.zeros((kv_groups, group_share, tok_count, HEAD_SIZE), jnp.float32),
     )
+    kv_width = keys.shape[1]
+    packed = jnp.concatenate(
+        [keys, values, jnp.pad(routes.astype(jnp.bfloat16), ((0, 0), (0, 128 - top_count)))], axis=1
+    )
+    gathered = lax.all_gather(packed, "ctx", axis=0, tiled=True)
+    all_routes = gathered[:, 2 * kv_width : 2 * kv_width + top_count].astype(jnp.int32)
     running_max, running_sum, weighted = fold_step(
         initial,
-        (
-            lax.all_gather(keys, "ctx", axis=0, tiled=True),
-            lax.all_gather(values, "ctx", axis=0, tiled=True),
-        ),
+        (gathered[:, :kv_width], gathered[:, kv_width : 2 * kv_width]),
         query_grid,
         tok_pos,
         tok_seg,
@@ -129,23 +119,33 @@
     own_hidden = lax.dynamic_slice_in_dim(hidden_in, row_start, own_rows, 0)
     residual = (own_hidden.astype(jnp.float32) + head_sums).astype(jnp.bfloat16)
     normed = rms_norm(residual, norm_gain)
-    own_routes = lax.dynamic_slice_in_dim(routes, row_start, own_rows, 0)
-    gates = gate_weights(normed, router, own_routes)
-    slot_ids = slot_index(own_routes, n_ctx, capacity)
-    placer = placer_matrix(slot_ids, n_ctx * capacity)
-    outgoing = jnp.dot(placer, normed, preferred_element_type=jnp.float32).astype(jnp.bfloat16)
-    arrived = lax.all_to_all(outgoing, "ctx", split_axis=0, concat_axis=0, tiled=True)
-    pieces = expert_piece(
-        lax.all_gather(arrived, "head", axis=0, tiled=True), w_gate_up, w_down
-    ).astype(jnp.float32)
-    summed = lax.psum_scatter(pieces.astype(jnp.bfloat16), "head", scatter_dimension=0, tiled=True)
-    returned = lax.all_to_all(summed, "ctx", split_axis=0, concat_axis=0, tiled=True)
-    match = (
-        slot_ids[:, :, None] == jnp.arange(n_ctx * capacity, dtype=jnp.int32)[None, None, :]
-    ).astype(jnp.float32)
-    combiner = jnp.sum(gates[:, :, None] * match, axis=1)
-    expert_mix = jnp.dot(combiner, returned.astype(jnp.float32), precision=lax.Precision.HIGHEST)
-    return (residual.astype(jnp.float32) + expert_mix).astype(jnp.bfloat16)
+    expert = lax.axis_index("ctx")
+    blocks = n_ctx * n_head
+    normed_all = lax.all_gather(normed, ("ctx", "head"), axis=0, tiled=True)
+    gate = expert_gates(normed_all, router, all_routes, expert).reshape(blocks, own_rows)
+    chosen = jnp.any(all_routes == expert, axis=1).reshape(blocks, own_rows)
+    rank = jnp.cumsum(chosen.astype(jnp.int32), axis=1) - 1
+    place = (
+        (rank[:, None, :] == jnp.arange(capacity, dtype=jnp.int32)[None, :, None])
+        & chosen[:, None, :]
+    )
+    token_rows = jnp.einsum(
+        "bcr,brd->bcd",
+        place.astype(jnp.bfloat16),
+        normed_all.reshape(blocks, own_rows, -1),
+        preferred_element_type=jnp.float32,
+    ).astype(jnp.bfloat16)
+    row_gate = jnp.sum(jnp.where(place, gate[:, None, :], 0.0), axis=2).reshape(-1, 1)
+    activation = expert_activation(token_rows.reshape(blocks * capacity, -1), w_gate_up)
+    pieces = jnp.dot(activation, w_down[0], preferred_element_type=jnp.float32)
+    gated = (pieces * row_gate).astype(jnp.bfloat16).reshape(blocks, capacity, -1)
+    spread = jnp.einsum(
+        "bcr,bcd->brd", place.astype(jnp.bfloat16), gated, preferred_element_type=jnp.float32
+    ).astype(jnp.bfloat16)
+    mixed = lax.psum_scatter(
+        spread.reshape(blocks * own_rows, -1), ("ctx", "head"), scatter_dimension=0, tiled=True
+    )
+    return (residual.astype(jnp.float32) + mixed.astype(jnp.float32)).astype(jnp.bfloat16)
 
 
 def solution(mesh):

time: 376 us -> 291 us (0.77)
  blocking collectives: 88.7 us -> 0 us
  other arithmetic: 7.75 us -> 14.3 us
  matrix products: 61 us -> 66.4 us
  starting transfers between devices: 4.87 us -> 0.31 us
  waiting for transfers between devices: 185 us -> 181 us
    all_to_all x1 -> x0, blocking collectives: 57 us -> none  [body(): lax.all_to_all(outgoing, 'ctx', split_axis=0, concat_axis=0, tiled=True)]
    all_to_all x1 -> x0, waiting for transfers between devices: 52 us -> none  [body(): lax.all_to_all(summed, 'ctx', split_axis=0, concat_axis=0, tiled=True)]
    all_gather x2 -> x0, blocking collectives: 31.6 us -> none  [the longest x1 16.8 us: body(): lax.all_gather(keys, 'ctx', axis=0, tiled=True)]
    all_gather x1 -> x2, waiting for transfers between devices: 58.5 us -> 83 us  [the longest x1 58.2 us: body(): normed_all = lax.all_gather(normed, ('ctx', 'head'), axis=0, tiled=True)]
    reduce_scatter x1, waiting for transfers between devices: 58.1 us -> 81.9 us  [body(): lax.psum_scatter(spread.reshape(blocks * own_rows, -1), ('ctx', 'head'),...]
    dot_general x5, matrix products: 41.4 us -> 50.7 us  [the longest x1 24.7 us: body(): pieces = jnp.dot(activation, w_down[0], preferred_element_type=jnp.float32)]
    convert_element_type x1 -> x5, other arithmetic: 0.01 us -> 5.23 us  [the longest x1 1.88 us: rms_norm(): return (widened * scale_rows * norm_gain).astype(jnp.bfloat16)]
    all_to_all x1 -> x0, starting transfers between devices: 4.61 us -> none  [body(): lax.all_to_all(summed, 'ctx', split_axis=0, concat_axis=0, tiled=True)]
  transfers between devices with their start and end apart: 4 -> 4, of which waited for: 4 -> 4; matrix products, arithmetic and copies ran while one was open for 1% -> 2% of each run, Pallas kernels for 0% -> 0%
where the time goes in v1:
time: 291 us
  waiting for transfers between devices  181 us (62%)
  matrix products  66.4 us (23%)
  local copies, waits for them, and re-layouts  15.5 us (5%)
  other arithmetic  14.3 us (5%)
  between operations  13.3 us (5%)
    reduce_scatter x1, waiting for transfers between devices, body(): lax.psum_scatter(spread.reshape(blocks * own_rows, -1), ('ctx', 'head'),...  81.9 us
    all_gather x1, waiting for transfers between devices, body(): normed_all = lax.all_gather(normed, ('ctx', 'head'), axis=0, tiled=True)  58.2 us
    all_gather x1, waiting for transfers between devices, body(): gathered = lax.all_gather(packed, 'ctx', axis=0, tiled=True)  24.8 us
    dot_general x1, matrix products, body(): pieces = jnp.dot(activation, w_down[0], preferred_element_type=jnp.float32)  24.7 us
    reduce_scatter x1, waiting for transfers between devices, body(): lax.psum_scatter(jnp.dot(attended, w_out, preferred_element_type=jnp.floa...  15.7 us
    dot_general x1, matrix products, expert_activation(): jnp.dot(token_rows, w_gate_up[0, 1], preferred_element_type=jnp.float32)  10.9 us
    dot_general x1, matrix products, body(): jnp.dot(attended, w_out, preferred_element_type=jnp.float32)  9.33 us
    dot_general x1, matrix products, body(): jnp.einsum('bcr,bcd->brd', place.astype(jnp.bfloat16), gated, preferred_e...  6.73 us
  transfers between devices with their start and end apart: 4, of which 4 were waited for; matrix products, arithmetic and copies ran while one was open for 2% of the time, Pallas kernels for 0%

profile of v1, /device:TPU:0, one launch (start us, length us, event | category | flops | bytes accessed | tf_op | source)
XLA Modules:
  0.0 290.6 jit_solution(8391737769341660964)
XLA Ops:
  6.5 0.8 convert_element_type.65
  7.3 0.9 copy.31
  8.2 1.0 copy.30
  9.2 0.7 fusion.41
  10.0 1.3 copy.32
  11.3 0.7 mul.77
  12.0 0.8 dynamic_slice.7
  12.8 0.9 fusion.32
  13.7 24.8 %all-gather.3.cloned.1.call-done = bf16[1024,640]{0,1:T(8,128)(2,1)} async-done(((bf16[128,640]{0,1:T(8,128)(2,1)}), bf16[1024,640]{0,1:T(8,128)(2,1)}) %all-gather.3.cloned.1.call-update) | async-done | bytes 1310736 | tf_op jit(solution)/shard_map/all_gather | solution.py:94
  38.5 1.3 fusion.50
  39.8 2.4 fusion
  42.3 4.1 %fusion.1 = f32[4,8,128]{2,1,0:T(8,128)S(1)} fusion(f32[4,1024,128,8]{2,1,3,0:T(8,128)S(1)} %get-tuple-element.10, f32[4,8,128]{2,1,0:T(8,128)S(1)} %broadcast_maximum_fusion, pred[128,1024]{0,1:T(8,128)(4,1)S(1)} %fusion.32), kind=kLoop, calls=%fused_computation.3 | loop fusion | flops 20967424 | bytes 16941056 | tf_op jit(solution)/shard_map/reduce_sum | solution.py:28
  46.5 3.9 %divide_convert_fusion = bf16[128,4,8,64]{0,3,2,1:T(8,128)(2,1)S(1)} fusion(bf16[1024,4,64,1]{0,2,3,1:T(8,128)(2,1)S(1)} %bitcast.77, f32[4,1024,128,8]{2,1,3,0:T(8,128)S(1)} %get-tuple-element.10, f32[4,8,128]{2,1,0:T(8,128)S(1)} %broadcast_maximum_fusion, pred[128,1024]{0,1:T(8,128)(4,1)S(1)} %fusion.32, f32[128,4,8]{0,2,1:T(8,128)S(1)} %get-tuple-element.8, ...), kind=kOutput, calls=%fused_computation.25 | convolution fusion | flops 558628864 | bytes 18006016 | tf_op jit(solution)/shard_map/cgtn,ncd->cgtd/dot_general | solution.py:29
  50.5 9.3 %convolution_convert_fusion.2 = bf16[128,2880]{1,0:T(8,128)(2,1)} fusion(bf16[128,2048]{0,1:T(8,128)(2,1)S(1)} %bitcast.76, bf16[2048,2880]{0,1:T(8,128)(2,1)} %param.19), kind=kOutput, calls=%fused_computation.19 | convolution fusion | flops 1510318080 | bytes 13058048 | tf_op jit(solution)/shard_map/dot_general | solution.py:114
  59.9 0.3 constant_dynamic-slice_fusion
  60.2 0.3 copy.38
  60.5 15.7 %reduce-scatter.3.cloned.1.call-done = bf16[64,2880]{1,0:T(8,128)(2,1)} async-done(((bf16[128,2880]{1,0:T(8,128)(2,1)}), bf16[64,2880]{1,0:T(8,128)(2,1)}) %reduce-scatter.3.cloned.1.call-update) | async-done | bytes 368656 | tf_op jit(solution)/shard_map/reduce_scatter | solution.py:113
  76.2 1.2 fusion.28
  77.4 1.9 fusion.30
  79.5 0.7 fusion.49
  80.6 0.7 slice_convert_fusion
  81.3 58.2 %all-gather.5.cloned.1.call-done = bf16[1024,2880]{1,0:T(8,128)(2,1)} async-done(((bf16[64,2880]{1,0:T(8,128)(2,1)}), bf16[1024,2880]{1,0:T(8,128)(2,1)}) %all-gather.5.cloned.1.call-update) | async-done | bytes 5898256 | tf_op jit(solution)/shard_map/all_gather | solution.py:124
  139.5 4.4 %fusion.51 = f32[1024,8]{0,1:T(8,128)S(1)} fusion(bf16[1024,2880]{1,0:T(8,128)(2,1)} %all-gather.5.cloned.1.call-done, bf16[2880,8]{0,1:T(8,128)(2,1)S(1)} %copy-done.4), kind=kOutput, calls=%fused_computation.66 | convolution fusion | flops 47185920 | bytes 5977088 | tf_op jit(solution)/shard_map/dot_general | solution.py:45
  144.0 0.7 fusion.42
  145.1 4.0 %convolution_convert_fusion.1 = bf16[16,48,2880]{2,1,0:T(8,128)(2,1)S(1)} fusion(bf16[16,64,2880]{2,1,0:T(8,128)(2,1)} %bitcast.69, s32[16,64]{1,0:T(8,128)S(1)} %broadcast_add_fusion, pred[16,64]{1,0:T(8,128)(4,1)S(1)} %reshape.77), kind=kOutput, calls=%fused_computation.17 | convolution fusion | flops 285425664 | bytes 10327040 | tf_op jit(solution)/shard_map/bcr,brd->bcd/dot_general | solution.py:132
  149.1 2.1 copy-done.2
  151.2 10.9 %fusion.5 = f32[768,1440]{0,1:T(8,128)} fusion(bf16[768,2880]{1,0:T(8,128)(2,1)S(1)} %bitcast.72, bf16[1,2,2880,1440]{2,3,1,0:T(8,128)(2,1)} %param.22), kind=kOutput, calls=%fused_computation.8 | convolution fusion | flops 6370099200 | bytes 17326080 | tf_op jit(solution)/shard_map/dot_general | solution.py:56
  162.1 24.7 %multiply_convert_fusion = bf16[768,2880]{0,1:T(8,128)(2,1)} fusion(bf16[1,1440,2880]{2,1,0:T(8,128)(2,1)} %param.23, f32[768]{0:T(1024)S(1)} %mul.95, f32[768,1440]{0,1:T(8,128)} %fusion.5, bf16[768,2880]{1,0:T(8,128)(2,1)} %bitcast.73, bf16[1,2,2880,1440]{2,3,1,0:T(8,128)(2,1)} %param.22), kind=kOutput, calls=%fused_computation.5 | convolution fusion | flops 12753469440 | bytes 30329856 | tf_op jit(solution)/shard_map/dot_general | solution.py:140
  186.8 6.6 %copy.34 = bf16[768,2880]{1,0:T(8,128)(2,1)} copy(bf16[768,2880]{0,1:T(8,128)(2,1)} %multiply_convert_fusion) | data formatting | bytes 8847360 | tf_op jit(solution)/shard_map/convert_element_type | solution.py:141
  193.5 6.7 %convolution_convert_fusion = bf16[16,64,2880]{2,1,0:T(8,128)(2,1)} fusion(bf16[16,48,2880]{2,1,0:T(8,128)(2,1)} %bitcast.71, s32[16,64]{1,0:T(8,128)S(1)} %broadcast_add_fusion, pred[16,64]{1,0:T(8,128)(4,1)S(1)} %reshape.77), kind=kOutput, calls=%fused_computation.16 | convolution fusion | flops 286162944 | bytes 10327040 | tf_op jit(solution)/shard_map/bcr,bcd->brd/dot_general | solution.py:142
  200.2 81.9 %reduce-scatter.5.cloned.1.call-done = bf16[64,2880]{1,0:T(8,128)(2,1)} async-done(((bf16[1024,2880]{1,0:T(8,128)(2,1)}), bf16[64,2880]{1,0:T(8,128)(2,1)}) %reduce-scatter.5.cloned.1.call-update) | async-done | bytes 368656 | tf_op jit(solution)/shard_map/reduce_scatter | solution.py:145
  282.2 1.9 fusion.31
  (33 shorter events, 1.3 us)
Async XLA Ops:
  6.5 53.4 %copy-start = (bf16[128,2880]{0,1:T(8,128)(2,1)S(1)}, bf16[128,2880]{0,1:T(8,128)(2,1)}, u32[]{:S(2)}) copy-start(bf16[128,2880]{0,1:T(8,128)(2,1)} %param.17) | copy-start | bytes 2211844
  6.5 32.0 %all-gather.3.cloned.1.call-start = ((), (), s32[]{:S(2)}) async-start(), calls=%async_computation.2 | async-start | bytes 1474560 | tf_op jit(solution)/shard_map/all_gather | solution.py:94
  9.9 66.2 %reduce-scatter.3.cloned.1.call-start = ((), (), s32[]{:S(2)}) async-start(), calls=%async_computation.3 | async-start | bytes 1130496 | tf_op jit(solution)/shard_map/reduce_scatter | solution.py:113
  50.5 26.9 %copy-start.5 = (f32[2880]{0:T(1024)S(1)}, f32[2880]{0:T(1024)}, u32[]{:S(2)}) copy-start(f32[2880]{0:T(1024)} %param.20) | copy-start | bytes 34564
  50.5 89.1 %copy-start.4 = (bf16[2880,8]{0,1:T(8,128)(2,1)S(1)}, bf16[2880,8]{0,1:T(8,128)(2,1)}, u32[]{:S(2)}) copy-start(bf16[2880,8]{0,1:T(8,128)(2,1)} %param.21) | copy-start | bytes 138244
  59.8 79.7 %all-gather.5.cloned.1.call-start = ((), (), s32[]{:S(2)}) async-start(), calls=%async_computation.4 | async-start | bytes 6406144 | tf_op jit(solution)/shard_map/all_gather | solution.py:124
  79.3 202.9 %reduce-scatter.5.cloned.1.call-start = ((), (), s32[]{:S(2)}) async-start(), calls=%async_computation.5 | async-start | bytes 6406144 | tf_op jit(solution)/shard_map/reduce_scatter | solution.py:145
  149.1 2.1 copy-start.2
  193.5 88.7 %copy-start.3 = (bf16[64,2880]{1,0:T(8,128)(2,1)S(1)}, bf16[64,2880]{1,0:T(8,128)(2,1)}, u32[]{:S(2)}) copy-start(bf16[64,2880]{1,0:T(8,128)(2,1)} %reduce-scatter.3.cloned.1.call-done) | copy-start | bytes 1105924
  193.5 90.6 %copy-start.1 = (bf16[128,2880]{0,1:T(8,128)(2,1)S(1)}, bf16[128,2880]{0,1:T(8,128)(2,1)}, u32[]{:S(2)}) copy-start(bf16[128,2880]{0,1:T(8,128)(2,1)} %param.17) | copy-start | bytes 2211844
Sparse Core Ops, SparseCore 0:
  10.0 28.4 all-gather.2
  60.0 16.1 reduce-scatter.2
  79.4 60.0 all-gather.4
  200.3 81.7 reduce-scatter.4

commit v2 on v1

--- a/solution.py
+++ b/solution.py
@@ -1,6 +1,10 @@
+import functools
+
 import jax
 import jax.numpy as jnp
 from jax import lax
+from jax.experimental import pallas as pl
+from jax.experimental.pallas import tpu as pltpu
 from jax.sharding import PartitionSpec as P
 
 HEAD_SIZE = 64
@@ -35,20 +39,369 @@
     return (new_max, running_sum, weighted)
 
 
-def rms_norm(residual, norm_gain):
-    widened = residual.astype(jnp.float32)
-    scale_rows = lax.rsqrt(jnp.mean(widened * widened, axis=-1, keepdims=True) + 1e-05)
-    return (widened * scale_rows * norm_gain).astype(jnp.bfloat16)
-
-
-def expert_gates(normed_rows, router, route_rows, expert):
-    logits = jnp.dot(normed_rows, router, preferred_element_type=jnp.float32)
-    onehot = (
-        route_rows[:, :, None] == jnp.arange(router.shape[1], dtype=jnp.int32)[None, None, :]
-    ).astype(jnp.float32)
-    picked = jnp.sum(onehot * logits[:, None, :], axis=-1)
-    gates = jax.nn.softmax(picked, axis=-1)
-    return jnp.sum(jnp.where(route_rows == expert, gates, 0.0), axis=1)
+MESH = pl.DeviceIdType.MESH
+LANES = 128
+CORES = 2
+
+
+def full_vmem():
+    return pl.BlockSpec(memory_space=pltpu.VMEM)
+
+
+class Ring:
+    def __init__(self, chips, heads):
+        self.chips, self.heads, self.count = chips, heads, chips * heads
+        ctx = lax.axis_index("ctx")
+        self.head = lax.axis_index("head")
+        self.core = lax.rem(ctx, CORES)
+        z = lax.div(ctx, CORES)
+        self.place = self.head * chips + z + lax.rem(self.head, 2) * (chips - 1 - 2 * z)
+        self.partner = {"ctx": z * CORES + 1 - self.core, "head": self.head}
+
+    def at(self, offset):
+        spot = lax.rem(self.place + offset + self.count, self.count)
+        head = lax.div(spot, self.chips)
+        step = lax.rem(spot, self.chips)
+        return head, step + lax.rem(head, 2) * (self.chips - 1 - 2 * step)
+
+    def block(self, offset, core):
+        head, z = self.at(offset)
+        return (z * CORES + core) * self.heads + head
+
+    def device(self, offset):
+        head, z = self.at(offset)
+        return {"ctx": z * CORES + self.core, "head": head}
+
+
+def remote(src, dst, send_sem, recv_sem, device):
+    return pltpu.make_async_remote_copy(
+        src_ref=src, dst_ref=dst, send_sem=send_sem, recv_sem=recv_sem, device_id=device, device_id_type=MESH
+    )
+
+
+def greet(devices):
+    barrier = pltpu.get_barrier_semaphore()
+    for device in devices:
+        pl.semaphore_signal(barrier, inc=1, device_id=device, device_id_type=MESH)
+    pl.semaphore_wait(barrier, len(devices))
+
+
+def row_chunks(rows):
+    if rows % 32 == 0:
+        return [pl.ds(0, rows // 2), pl.ds(rows // 2, rows // 2)]
+    return [pl.ds(0, rows)]
+
+
+def line_kernel(chips, key_ref, value_ref, all_keys, all_values, line_send, line_recv, pair_send, pair_recv, own_sem):
+    ctx = lax.axis_index("ctx")
+    z, core = lax.div(ctx, CORES), lax.rem(ctx, CORES)
+    ins, outs = (key_ref, value_ref), (all_keys, all_values)
+    partner = {"ctx": z * CORES + 1 - core}
+    ways = ((0, 1), (1, -1))
+
+    def inside(spot):
+        return (spot >= 0) & (spot < chips)
+
+    barrier = pltpu.get_barrier_semaphore()
+    pl.semaphore_signal(barrier, inc=1, device_id=partner, device_id_type=MESH)
+    for _, way in ways:
+
+        @pl.when(inside(z + way))
+        def _():
+            pl.semaphore_signal(
+                barrier, inc=1, device_id={"ctx": (z + way) * CORES + core}, device_id_type=MESH
+            )
+
+    peers = 1 + sum(jnp.where(inside(z + way), 1, 0) for _, way in ways)
+    pl.semaphore_wait(barrier, peers)
+
+    def hop(index, way, step, part):
+        block = (z - way * step) * CORES + core
+        source = ins[part] if step == 0 else outs[part].at[block]
+        return remote(
+            source,
+            outs[part].at[block],
+            line_send.at[index, step, part],
+            line_recv.at[index, step, part],
+            {"ctx": (z + way) * CORES + core},
+        )
+
+    def share(slot, block, part):
+        source = ins[part] if slot == 0 else outs[part].at[block]
+        return remote(source, outs[part].at[block], pair_send.at[slot, part], pair_recv.at[slot, part], partner)
+
+    def keep(part):
+        return pltpu.make_async_copy(ins[part], outs[part].at[ctx], own_sem.at[part])
+
+    for part in (0, 1):
+        for index, way in ways:
+
+            @pl.when(inside(z + way))
+            def _():
+                hop(index, way, 0, part).start()
+
+    for part in (0, 1):
+        share(0, ctx, part).start()
+        keep(part).start()
+    for step in range(1, chips):
+        for part in (0, 1):
+            for index, way in ways:
+
+                @pl.when(inside(z - way * step))
+                def _():
+                    hop(index, way, step - 1, part).wait_recv()
+                    if step < chips - 1:
+
+                        @pl.when(inside(z + way))
+                        def _():
+                            hop(index, way, step, part).start()
+
+                    share(index * (chips - 1) + step, (z - way * step) * CORES + core, part).start()
+
+    for part in (0, 1):
+        keep(part).wait()
+        share(0, ctx, part).wait()
+        for index, way in ways:
+            for step in range(chips):
+                if step < chips - 1:
+
+                    @pl.when(inside(z + way) & inside(z - way * step))
+                    def _():
+                        hop(index, way, step, part).wait_send()
+
+                if step > 0:
+
+                    @pl.when(inside(z - way * step))
+                    def _():
+                        share(index * (chips - 1) + step, (z - way * step) * CORES + core, part).wait()
+
+
+def gather_keys(keys, values):
+    n_ctx = lax.axis_size("ctx")
+    chips = n_ctx // CORES
+    shape = jax.ShapeDtypeStruct((n_ctx,) + keys.shape, keys.dtype)
+    slots = 2 * (chips - 1) + 1
+    gathered = pl.pallas_call(
+        functools.partial(line_kernel, chips),
+        out_shape=(shape, shape),
+        in_specs=[full_vmem()] * 2,
+        out_specs=(full_vmem(),) * 2,
+        scratch_shapes=[
+            pltpu.SemaphoreType.DMA((2, chips, 2)),
+            pltpu.SemaphoreType.DMA((2, chips, 2)),
+            pltpu.SemaphoreType.DMA((slots, 2)),
+            pltpu.SemaphoreType.DMA((slots, 2)),
+            pltpu.SemaphoreType.DMA((2,)),
+        ],
+        compiler_params=pltpu.CompilerParams(collective_id=0, has_side_effects=True),
+        name="gather_keys",
+    )(keys, values)
+    return [array.reshape(-1, array.shape[-1]) for array in gathered]
+
+
+def norm_kernel(
+    chips, heads, experts, part_ref, hidden_ref, gain_ref, router_ref, route_ref, residual_ref, all_ref,
+    slots, head_send, head_recv, ring_send, ring_recv, pair_send, pair_recv,
+):
+    ring = Ring(chips, heads)
+    count, half = ring.count, ring.count // 2
+    rows, width = hidden_ref.shape
+    ctx, head = lax.axis_index("ctx"), ring.head
+    others = [{"ctx": ctx, "head": lax.rem(head + turn, heads)} for turn in range(1, heads)]
+    greet([ring.device(1), ring.device(-1), ring.partner] + others)
+
+    sends = []
+    for turn, device in enumerate(others):
+        target = pl.ds(pl.multiple_of(device["head"] * rows, rows), rows)
+        copy = remote(part_ref.at[target], slots.at[turn], head_send.at[turn], head_recv.at[turn], device)
+        copy.start()
+        sends.append(copy)
+    own = pl.ds(pl.multiple_of(head * rows, rows), rows)
+    total = hidden_ref[...].astype(jnp.float32) + part_ref[own, :].astype(jnp.float32)
+    for turn, copy in enumerate(sends):
+        copy.wait_recv()
+        total = total + slots[turn].astype(jnp.float32)
+    residual = total.astype(jnp.bfloat16)
+    residual_ref[...] = residual
+    wide = residual.astype(jnp.float32)
+    scale = lax.rsqrt(jnp.mean(wide * wide, axis=-1, keepdims=True) + 1e-05)
+    normed = (wide * scale * gain_ref[...]).astype(jnp.bfloat16)
+
+    logits = lax.dot_general(
+        normed, router_ref[...], (((1,), (1,)), ((), ())), preferred_element_type=jnp.float32
+    )
+    start = width % LANES
+    lane = lax.broadcasted_iota(jnp.int32, logits.shape, 1) - start
+    first = (lane >= 0) & (lane < experts)
+    present = jnp.zeros(logits.shape, jnp.bool_)
+    for k in range(route_ref.shape[1]):
+        route = route_ref[:, k : k + 1]
+        present = present | (lane == route) | (lane - experts == route)
+    top = jnp.max(jnp.where(present, logits, -jnp.inf), axis=-1, keepdims=True)
+    powers = jnp.where(present, jnp.exp(jnp.where(present, logits - top, 0.0)), 0.0)
+    gates = powers / jnp.sum(jnp.where(first, powers, 0.0), axis=-1, keepdims=True)
+    coarse = gates.astype(jnp.bfloat16)
+    rest = gates - coarse.astype(jnp.float32)
+    mine = ring.block(0, ring.core)
+    all_ref[mine, :, width - start :] = jnp.where(first, coarse.astype(jnp.float32), rest).astype(jnp.bfloat16)
+    all_ref[mine, :, :width] = normed
+
+    chunks = row_chunks(rows)
+    hops, shares = {}, []
+
+    def share(slot, block, j):
+        view = all_ref.at[block, chunks[j]]
+        copy = remote(view, view, pair_send.at[slot, j], pair_recv.at[slot, j], ring.partner)
+        copy.start()
+        shares.append(copy)
+
+    for step in range(half + 1):
+        for j in range(len(chunks)):
+            for index, way in ((0, 1), (1, -1)):
+                block = ring.block(-way * step, ring.core)
+                if step > 0 and (index, step - 1, j) in hops:
+                    hops[index, step - 1, j].wait_recv()
+                if step < half - 1 or (step == half - 1 and (j == 0) == (index == 0)):
+                    view = all_ref.at[block, chunks[j]]
+                    hops[index, step, j] = remote(
+                        view, view, ring_send.at[index, step, j], ring_recv.at[index, step, j], ring.device(way)
+                    )
+                    hops[index, step, j].start()
+                if step == 0 and index == 0:
+                    share(0, block, j)
+                elif step > 0 and (index, step - 1, j) in hops:
+                    share(index * half + step, block, j)
+    for copy in sends + list(hops.values()):
+        copy.wait_send()
+    for copy in shares:
+        copy.wait()
+
+
+def norm_and_gather(partial_sums, own_hidden, norm_gain, router, own_routes):
+    chips, heads = lax.axis_size("ctx") // CORES, lax.axis_size("head")
+    rows, width = own_hidden.shape
+    experts = router.shape[1]
+    start = width % LANES
+    padded = width - start + LANES
+    half = chips * heads // 2
+    parts = len(row_chunks(rows))
+    turned = router.T
+    lanes = jnp.concatenate(
+        [
+            jnp.zeros((start, width), router.dtype),
+            turned,
+            turned,
+            jnp.zeros((LANES - start - 2 * experts, width), router.dtype),
+        ],
+        axis=0,
+    )
+    return pl.pallas_call(
+        functools.partial(norm_kernel, chips, heads, experts),
+        out_shape=(
+            jax.ShapeDtypeStruct((rows, width), jnp.bfloat16),
+            jax.ShapeDtypeStruct((chips * heads * CORES, rows, padded), jnp.bfloat16),
+        ),
+        in_specs=[full_vmem()] * 5,
+        out_specs=(full_vmem(),) * 2,
+        scratch_shapes=[
+            pltpu.VMEM((heads - 1, rows, width), jnp.bfloat16),
+            pltpu.SemaphoreType.DMA((heads - 1,)),
+            pltpu.SemaphoreType.DMA((heads - 1,)),
+            pltpu.SemaphoreType.DMA((2, half, parts)),
+            pltpu.SemaphoreType.DMA((2, half, parts)),
+            pltpu.SemaphoreType.DMA((2 * half + 1, parts)),
+            pltpu.SemaphoreType.DMA((2 * half + 1, parts)),
+        ],
+        compiler_params=pltpu.CompilerParams(collective_id=1, has_side_effects=True),
+        name="norm_and_gather",
+    )(partial_sums, own_hidden, norm_gain.reshape(1, -1), lanes, own_routes)
+
+
+def sum_kernel(
+    chips, heads, term_ref, residual_ref, out_ref,
+    got, outgoing, incoming, pair_send, pair_recv, ring_send, ring_recv,
+):
+    ring = Ring(chips, heads)
+    half = ring.count // 2
+    chunks = row_chunks(residual_ref.shape[0])
+    greet([ring.device(1), ring.device(-1), ring.partner])
+    order = [half]
+    for distance in range(half - 1, 0, -1):
+        order += [distance, -distance]
+    order.append(0)
+    shares = {}
+    for slot, offset in enumerate(order):
+        shares[offset] = remote(
+            term_ref.at[ring.block(offset, 1 - ring.core)],
+            got.at[slot],
+            pair_send.at[slot],
+            pair_recv.at[slot],
+            ring.partner,
+        )
+        shares[offset].start()
+    arrived = set()
+
+    def pair(offset, chunk):
+        if offset == -half:
+            offset = half
+        if offset not in arrived:
+            shares[offset].wait_recv()
+            arrived.add(offset)
+        mine = term_ref[ring.block(offset, ring.core), chunk, :].astype(jnp.float32)
+        return mine + got[order.index(offset), chunk, :].astype(jnp.float32)
+
+    hops = {}
+    for step in range(half):
+        for j, chunk in enumerate(chunks):
+            for index, way in ((0, 1), (1, -1)):
+                if step == 0 and (j == 0) != (index == 0):
+                    continue
+                total = pair(way * (half - step), chunk)
+                if (index, step - 1, j) in hops:
+                    hops[index, step - 1, j].wait_recv()
+                    total = total + incoming[index, step - 1, chunk, :].astype(jnp.float32)
+                outgoing[index, step, chunk, :] = total.astype(jnp.bfloat16)
+                hops[index, step, j] = remote(
+                    outgoing.at[index, step, chunk],
+                    incoming.at[index, step, chunk],
+                    ring_send.at[index, step, j],
+                    ring_recv.at[index, step, j],
+                    ring.device(way),
+                )
+                hops[index, step, j].start()
+    for j, chunk in enumerate(chunks):
+        total = pair(0, chunk) + residual_ref[chunk, :].astype(jnp.float32)
+        for index in (0, 1):
+            if (index, half - 1, j) in hops:
+                hops[index, half - 1, j].wait_recv()
+                total = total + incoming[index, half - 1, chunk, :].astype(jnp.float32)
+        out_ref[chunk, :] = total.astype(jnp.bfloat16)
+    for copy in list(shares.values()) + list(hops.values()):
+        copy.wait_send()
+
+
+def sum_and_scatter(terms, residual):
+    chips, heads = lax.axis_size("ctx") // CORES, lax.axis_size("head")
+    rows, width = residual.shape
+    half = chips * heads // 2
+    parts = len(row_chunks(rows))
+    return pl.pallas_call(
+        functools.partial(sum_kernel, chips, heads),
+        out_shape=jax.ShapeDtypeStruct((rows, width), jnp.bfloat16),
+        in_specs=[full_vmem()] * 2,
+        out_specs=full_vmem(),
+        scratch_shapes=[
+            pltpu.VMEM((2 * half, rows, width), jnp.bfloat16),
+            pltpu.VMEM((2, half, rows, width), jnp.bfloat16),
+            pltpu.VMEM((2, half, rows, width), jnp.bfloat16),
+            pltpu.SemaphoreType.DMA((2 * half,)),
+            pltpu.SemaphoreType.DMA((2 * half,)),
+            pltpu.SemaphoreType.DMA((2, half, parts)),
+            pltpu.SemaphoreType.DMA((2, half, parts)),
+        ],
+        compiler_params=pltpu.CompilerParams(collective_id=2, has_side_effects=True),
+        name="sum_and_scatter",
+    )(terms, residual)
 
 
 def expert_activation(token_rows, w_gate_up):
@@ -87,15 +440,10 @@
         jnp.ones_like(sink_grid),
         jnp.zeros((kv_groups, group_share, tok_count, HEAD_SIZE), jnp.float32),
     )
-    kv_width = keys.shape[1]
-    packed = jnp.concatenate(
-        [keys, values, jnp.pad(routes.astype(jnp.bfloat16), ((0, 0), (0, 128 - top_count)))], axis=1
-    )
-    gathered = lax.all_gather(packed, "ctx", axis=0, tiled=True)
-    all_routes = gathered[:, 2 * kv_width : 2 * kv_width + top_count].astype(jnp.int32)
+    all_keys, all_values = gather_keys(keys, values)
     running_max, running_sum, weighted = fold_step(
         initial,
-        (gathered[:, :kv_width], gathered[:, kv_width : 2 * kv_width]),
+        (all_keys, all_values),
         query_grid,
         tok_pos,
         tok_seg,
@@ -110,20 +458,24 @@
     own_rows = tok_count // n_head
     row_start = lax.axis_index("head") * own_rows
     capacity = max(2, min(tok_count // n_head, 3 * tok_count * top_count // (2 * n_head * n_ctx)))
-    head_sums = lax.psum_scatter(
-        jnp.dot(attended, w_out, preferred_element_type=jnp.float32).astype(jnp.bfloat16),
-        "head",
-        scatter_dimension=0,
-        tiled=True,
-    ).astype(jnp.float32)
+    partial_sums = jnp.dot(attended, w_out, preferred_element_type=jnp.float32).astype(jnp.bfloat16)
     own_hidden = lax.dynamic_slice_in_dim(hidden_in, row_start, own_rows, 0)
-    residual = (own_hidden.astype(jnp.float32) + head_sums).astype(jnp.bfloat16)
-    normed = rms_norm(residual, norm_gain)
+    own_routes = lax.dynamic_slice_in_dim(routes, row_start, own_rows, 0)
+    residual, gathered = norm_and_gather(partial_sums, own_hidden, norm_gain, router, own_routes)
+    width, experts = router.shape
     expert = lax.axis_index("ctx")
     blocks = n_ctx * n_head
-    normed_all = lax.all_gather(normed, ("ctx", "head"), axis=0, tiled=True)
-    gate = expert_gates(normed_all, router, all_routes, expert).reshape(blocks, own_rows)
-    chosen = jnp.any(all_routes == expert, axis=1).reshape(blocks, own_rows)
+    normed_all = gathered[:, :, :width]
+    lanes = jnp.arange(2 * experts, dtype=jnp.int32)
+    gate = jnp.sum(
+        jnp.where(
+            (lanes == expert) | (lanes == expert + experts),
+            gathered[:, :, width : width + 2 * experts].astype(jnp.float32),
+            0.0,
+        ),
+        axis=-1,
+    )
+    chosen = gate > 0.0
     rank = jnp.cumsum(chosen.astype(jnp.int32), axis=1) - 1
     place = (
         (rank[:, None, :] == jnp.arange(capacity, dtype=jnp.int32)[None, :, None])
@@ -132,7 +484,7 @@
     token_rows = jnp.einsum(
         "bcr,brd->bcd",
         place.astype(jnp.bfloat16),
-        normed_all.reshape(blocks, own_rows, -1),
+        normed_all,
         preferred_element_type=jnp.float32,
     ).astype(jnp.bfloat16)
     row_gate = jnp.sum(jnp.where(place, gate[:, None, :], 0.0), axis=2).reshape(-1, 1)
@@ -142,10 +494,7 @@
     spread = jnp.einsum(
         "bcr,bcd->brd", place.astype(jnp.bfloat16), gated, preferred_element_type=jnp.float32
     ).astype(jnp.bfloat16)
-    mixed = lax.psum_scatter(
-        spread.reshape(blocks * own_rows, -1), ("ctx", "head"), scatter_dimension=0, tiled=True
-    )
-    return (residual.astype(jnp.float32) + mixed.astype(jnp.float32)).astype(jnp.bfloat16)
+    return sum_and_scatter(spread, residual)
 
 
 def solution(mesh):

time: 291 us -> 205 us (0.70)
  waiting for transfers between devices: 181 us -> 0 us
  Pallas kernels: 0 us -> 107 us
  between operations: 13.3 us -> 0.2 us
    pallas_call x0 -> x3, Pallas kernels: none -> 107 us  [the longest x1 48.9 us: norm_and_gather(): pl.pallas_call(functools.partial(norm_kernel, chips, heads, experts), out...]
    reduce_scatter x2 -> x0, waiting for transfers between devices: 97.6 us -> none  [the longest x1 81.9 us: body(): lax.psum_scatter(spread.reshape(blocks * own_rows, -1), ('ctx', 'head'),...]
    all_gather x2 -> x0, waiting for transfers between devices: 83 us -> none  [the longest x1 58.2 us: body(): normed_all = lax.all_gather(normed, ('ctx', 'head'), axis=0, tiled=True)]
    convert_element_type x4 -> x0, other arithmetic: 5.22 us -> none  [the longest x1 1.88 us: rms_norm(): return (widened * scale_rows * norm_gain).astype(jnp.bfloat16)]
    dot_general x1, matrix products: 2.4 us -> 7.04 us  [fold_step(): jnp.einsum('tcgd,ncd->cgtn', query_grid, key_grid, preferred_element_type...]
    dot_general x2 -> x1, matrix products: 8.39 us -> 4.04 us  [body(): jnp.einsum('bcr,brd->bcd', place.astype(jnp.bfloat16), normed_all, prefer...]
    dot_general x1, matrix products: 3.94 us -> 7.84 us  [fold_step(): jnp.einsum('cgtn,ncd->cgtd', weights.astype(jnp.bfloat16), value_grid, pr...]
    reduce_sum x1, other arithmetic: 4.15 us -> 8.03 us  [fold_step(): running_sum = running_sum * rescale + jnp.sum(weights, axis=-1)]
  transfers between devices with their start and end apart: 4 -> 0, of which waited for: 4 -> 0; matrix products, arithmetic and copies ran while one was open for 2% -> 0% of each run, Pallas kernels for 0% -> 0%
where the time goes in v2:
time: 205 us; the launch traced here: 204 us
  Pallas kernels  107 us (52%)
  matrix products  69.1 us (34%)
  local copies, waits for them, and re-layouts  16.6 us (8%)
  other arithmetic  11.8 us (6%)
    pallas_call x1, Pallas kernels, norm_and_gather(): pl.pallas_call(functools.partial(norm_kernel, chips, heads, experts), out...  48.9 us
    pallas_call x1, Pallas kernels, sum_and_scatter(): pl.pallas_call(functools.partial(sum_kernel, chips, heads), out_shape=jax...  39.1 us
    dot_general x1, matrix products, body(): pieces = jnp.dot(activation, w_down[0], preferred_element_type=jnp.float32)  24.8 us
    pallas_call x1, Pallas kernels, gather_keys(): pl.pallas_call(functools.partial(line_kernel, chips), out_shape=(shape, s...  18.6 us
    dot_general x1, matrix products, expert_activation(): jnp.dot(token_rows, w_gate_up[0, 1], preferred_element_type=jnp.float32)  12.5 us
    reduce_sum x1, other arithmetic, fold_step(): running_sum = running_sum * rescale + jnp.sum(weights, axis=-1)  8.03 us
    dot_general x1, matrix products, fold_step(): jnp.einsum('cgtn,ncd->cgtd', weights.astype(jnp.bfloat16), value_grid, pr...  7.84 us
    dot_general x1, matrix products, fold_step(): jnp.einsum('tcgd,ncd->cgtn', query_grid, key_grid, preferred_element_type...  7.04 us

profile of v2, /device:TPU:0, one launch (start us, length us, event | category | flops | bytes accessed | tf_op | source)
XLA Modules:
  0.0 204.4 jit_solution(11192694713044102228)
XLA Ops:
  0.0 0.8 dynamic_slice.9
  0.8 0.9 fusion.36
  1.7 18.6 %gather_keys.1 = (bf16[8,128,256]{2,1,0:T(8,128)(2,1)}, bf16[8,128,256]{2,1,0:T(8,128)(2,1)}) custom-call(bf16[128,256]{1,0:T(8,128)(2,1)} %key_ref.1, bf16[128,256]{1,0:T(8,128)(2,1)} %value_ref.1), custom_call_target="tpu_custom_call" | custom-call | tf_op jit(solution)/shard_map/gather_keys/pallas_call | solution.py:184
  20.4 1.4 copy.29
  21.8 0.2 reshape.54
  22.0 1.3 copy.30
  23.3 7.0 %fusion = (f32[4,8,128]{2,1,0:T(8,128)S(1)}, f32[4,1024,128,8]{2,1,3,0:T(8,128)}) fusion(pred[128,1024]{0,1:T(8,128)(4,1)S(1)} %fusion.36, bf16[128,4,8,64]{0,3,2,1:T(8,128)(2,1)S(1)} %bitcast.68, bf16[1024,4,64,1]{0,2,1,3:T(8,128)(2,1)S(1)} %reshape.54), kind=kOutput, calls=%fused_computation.2 | convolution fusion | flops 549449728 | bytes 17973248 | tf_op jit(solution)/shard_map/tcgd,ncd->cgtn/dot_general | solution.py:23
  30.4 0.1 mul.49
  30.5 8.0 %fusion.1 = f32[4,8,128]{2,1,0:T(8,128)S(1)} fusion(f32[4,1024,128,8]{2,1,3,0:T(8,128)} %get-tuple-element.18, f32[4,8,128]{2,1,0:T(8,128)S(1)} %broadcast_maximum_fusion, pred[128,1024]{0,1:T(8,128)(4,1)S(1)} %fusion.36), kind=kLoop, calls=%fused_computation.3 | loop fusion | flops 20967424 | bytes 16941056 | tf_op jit(solution)/shard_map/reduce_sum | solution.py:32
  38.6 0.1 multiply_bitcast_fusion
  38.7 0.3 copy.31
  39.0 0.2 reshape.55
  39.2 7.8 %divide_convert_fusion = bf16[128,4,8,64]{0,3,2,1:T(8,128)(2,1)S(1)} fusion(f32[4,1024,128,8]{2,1,3,0:T(8,128)} %get-tuple-element.18, f32[4,8,128]{2,1,0:T(8,128)S(1)} %broadcast_maximum_fusion, pred[128,1024]{0,1:T(8,128)(4,1)S(1)} %fusion.36, bf16[1024,4,64,1]{0,2,1,3:T(8,128)(2,1)S(1)} %reshape.55, f32[128,4,8]{0,2,1:T(8,128)S(1)} %get-tuple-element.16, ...), kind=kOutput, calls=%fused_computation.24 | convolution fusion | flops 558628864 | bytes 18006016 | tf_op jit(solution)/shard_map/cgtn,ncd->cgtd/dot_general | solution.py:33
  47.1 6.2 %convolution_convert_fusion.1 = bf16[128,2880]{0,1:T(8,128)(2,1)S(1)} fusion(bf16[2048,2880]{0,1:T(8,128)(2,1)} %param.19, bf16[128,2048]{0,1:T(8,128)(2,1)S(1)} %bitcast.70), kind=kOutput, calls=%fused_computation.21 | convolution fusion | flops 1510318080 | bytes 13058048 | tf_op jit(solution)/shard_map/dot_general | solution.py:461
  53.3 1.2 copy.35.part_ref
  54.5 0.3 constant_dynamic-slice_fusion.1
  54.7 1.0 copy.40.hidden_ref
  55.8 0.7 copy.41.route_ref
  56.5 0.1 pad.3.clone
  56.6 1.0 maximum_maximum_fusion.router_ref
  57.6 0.6 reshape.51.gain_ref
  58.2 48.9 %norm_and_gather.1 = (bf16[64,2880]{1,0:T(8,128)(2,1)}, bf16[16,64,2944]{2,1,0:T(8,128)(2,1)}) custom-call(bf16[128,2880]{1,0:T(8,128)(2,1)} %copy.35.part_ref, bf16[64,2880]{1,0:T(8,128)(2,1)} %copy.40.hidden_ref, f32[1,2880]{1,0:T(1,128)} %reshape.51.gain_ref, bf16[128,2880]{1,0:T(8,128)(2,1)} %maximum_maximum_fusion.router_ref, s32[64,4]{1,0:T(8,128)} %copy.41.route_ref), custom_call_target="tpu_custom_call" | custom-call | tf_op jit(solution)/shard_map/norm_and_gather/pallas_call | solution.py:298
  107.1 1.3 select_reduce_fusion
  108.4 0.2 reduce_window_sum.11
  108.7 4.0 %fusion.18 = bf16[16,48,2880]{2,1,0:T(8,128)(2,1)S(1)} fusion(bf16[16,64,2944]{2,1,0:T(8,128)(2,1)} %get-tuple-element.11, s32[16,64]{1,0:T(8,128)S(1)} %broadcast_add_fusion, pred[16,64]{1,0:T(8,128)(4,1)S(1)} %get-tuple-element.14), kind=kOutput, calls=%fused_computation.19 | convolution fusion | flops 285425664 | bytes 10458112 | tf_op jit(solution)/shard_map/bcr,brd->bcd/dot_general | solution.py:484
  112.7 12.5 %fusion.5 = f32[768,1440]{0,1:T(8,128)} fusion(bf16[768,2880]{1,0:T(8,128)(2,1)S(1)} %bitcast.66, bf16[1,2,2880,1440]{2,3,1,0:T(8,128)(2,1)} %param.22), kind=kOutput, calls=%fused_computation.8 | convolution fusion | flops 6370099200 | bytes 17326080 | tf_op jit(solution)/shard_map/dot_general | solution.py:409
  125.2 0.2 select_reduce_fusion.1
  125.5 24.8 %multiply_convert_fusion = bf16[768,2880]{0,1:T(8,128)(2,1)} fusion(bf16[1,1440,2880]{2,1,0:T(8,128)(2,1)} %param.23, f32[768]{0:T(1024)S(1)} %mul.61, f32[768,1440]{0,1:T(8,128)} %fusion.5, bf16[768,2880]{1,0:T(8,128)(2,1)} %bitcast.67, bf16[1,2,2880,1440]{2,3,1,0:T(8,128)(2,1)} %param.22), kind=kOutput, calls=%fused_computation.5 | convolution fusion | flops 12753469440 | bytes 30329856 | tf_op jit(solution)/shard_map/dot_general | solution.py:492
  150.3 6.5 %copy.36 = bf16[768,2880]{1,0:T(8,128)(2,1)} copy(bf16[768,2880]{0,1:T(8,128)(2,1)} %multiply_convert_fusion) | data formatting | bytes 8847360 | tf_op jit(solution)/shard_map/convert_element_type | solution.py:493
  156.8 6.7 %convolution_convert_fusion.term_ref = bf16[16,64,2880]{2,1,0:T(8,128)(2,1)} fusion(bf16[16,48,2880]{2,1,0:T(8,128)(2,1)} %bitcast.65, s32[16,64]{1,0:T(8,128)S(1)} %broadcast_add_fusion, pred[16,64]{1,0:T(8,128)(4,1)S(1)} %get-tuple-element.14), kind=kOutput, calls=%fused_computation.18 | convolution fusion | flops 286162944 | bytes 10327040 | tf_op jit(solution)/shard_map/bcr,bcd->brd/dot_general | solution.py:494
  163.5 39.1 %sum_and_scatter.1 = bf16[64,2880]{1,0:T(8,128)(2,1)} custom-call(bf16[16,64,2880]{2,1,0:T(8,128)(2,1)} %convolution_convert_fusion.term_ref, bf16[64,2880]{1,0:T(8,128)(2,1)} %get-tuple-element.12.residual_ref), custom_call_target="tpu_custom_call" | custom-call | tf_op jit(solution)/shard_map/sum_and_scatter/pallas_call | solution.py:388
  202.6 1.8 copy.43
  (26 shorter events, 0.3 us)
Async XLA Ops:
  0.0 54.5 %copy-start = (bf16[128,2880]{0,1:T(8,128)(2,1)S(1)}, bf16[128,2880]{0,1:T(8,128)(2,1)}, u32[]{:S(2)}) copy-start(bf16[128,2880]{0,1:T(8,128)(2,1)} %param.17) | copy-start | bytes 2211844
  23.3 7.1 %copy-start.7 = (f32[32]{0:T(128)S(1)}, f32[32]{0:T(128)}, u32[]{:S(2)}) copy-start(f32[32]{0:T(128)} %param.15) | copy-start | bytes 388
  30.5 8.1 %copy-start.3 = (bf16[8,128,256]{2,1,0:T(8,128)(2,1)S(1)}, bf16[8,128,256]{2,1,0:T(8,128)(2,1)}, u32[]{:S(2)}) copy-start(bf16[8,128,256]{2,1,0:T(8,128)(2,1)} %get-tuple-element.10) | copy-start | bytes 1572868
  47.1 8.7 %copy-start.6 = (s32[128,4]{0,1:T(4,128)S(1)}, s32[128,4]{0,1:T(4,128)}, u32[]{:S(2)}) copy-start(s32[128,4]{0,1:T(4,128)} %param.18) | copy-start | bytes 6148
  47.1 9.5 %copy-start.4 = (bf16[2880,8]{0,1:T(8,128)(2,1)S(1)}, bf16[2880,8]{0,1:T(8,128)(2,1)}, u32[]{:S(2)}) copy-start(bf16[2880,8]{0,1:T(8,128)(2,1)} %param.21) | copy-start | bytes 138244
  47.1 10.5 %copy-start.5 = (f32[2880]{0:T(1024)S(1)}, f32[2880]{0:T(1024)}, u32[]{:S(2)}) copy-start(f32[2880]{0:T(1024)} %param.20) | copy-start | bytes 34564
  112.7 12.5 %copy-start.2 = (bf16[16,48,2880]{2,1,0:T(8,128)(2,1)}, bf16[16,48,2880]{2,1,0:T(8,128)(2,1)S(1)}, u32[]{:S(2)}) copy-start(bf16[16,48,2880]{2,1,0:T(8,128)(2,1)S(1)} %fusion.18) | copy-start | bytes 13271044
  156.8 47.6 %copy-start.1 = (bf16[128,2880]{0,1:T(8,128)(2,1)S(1)}, bf16[128,2880]{0,1:T(8,128)(2,1)}, u32[]{:S(2)}) copy-start(bf16[128,2880]{0,1:T(8,128)(2,1)} %param.17) | copy-start | bytes 2211844

commit v3 on v2

--- a/solution.py
+++ b/solution.py
@@ -317,20 +317,121 @@
     )(partial_sums, own_hidden, norm_gain.reshape(1, -1), lanes, own_routes)
 
 
-def sum_kernel(
-    chips, heads, term_ref, residual_ref, out_ref,
-    got, outgoing, incoming, pair_send, pair_recv, ring_send, ring_recv,
+def row_placement(tail, expert, experts, start, capacity):
+    rows = tail.shape[0]
+    lane = lax.broadcasted_iota(jnp.int32, (LANES, tail.shape[1]), 1) - start
+    pick = ((lane == expert) | (lane == expert + experts)).astype(jnp.float32).astype(jnp.bfloat16)
+    spot = lax.broadcasted_iota(jnp.int32, (rows, rows), 0)
+    other = lax.broadcasted_iota(jnp.int32, (rows, rows), 1)
+    turned = (((1,), (1,)), ((), ()))
+    across = lax.dot_general(pick, tail, turned, preferred_element_type=jnp.float32)
+    before = (spot < other).astype(jnp.float32).astype(jnp.bfloat16)
+    named = (across > 0.0).astype(jnp.float32)
+    rank = jnp.dot(named.astype(jnp.bfloat16), before, preferred_element_type=jnp.float32)
+    slot = lax.broadcasted_iota(jnp.int32, (capacity, rows), 0)
+    match = (rank[:1] == slot.astype(jnp.float32)) & (named[:1] > 0.0)
+    gate = jnp.sum(jnp.where(match, across[:1], 0.0), axis=1, keepdims=True)
+    down = lax.dot_general(tail, pick, turned, preferred_element_type=jnp.float32)
+    named_down = (down > 0.0).astype(jnp.float32)
+    after = (spot > other).astype(jnp.float32).astype(jnp.bfloat16)
+    rank_down = jnp.dot(after, named_down.astype(jnp.bfloat16), preferred_element_type=jnp.float32)
+    slot_down = lax.broadcasted_iota(jnp.int32, (rows, capacity), 1)
+    match_down = (rank_down[:, :1] == slot_down.astype(jnp.float32)) & (named_down[:, :1] > 0.0)
+    return (
+        match.astype(jnp.float32).astype(jnp.bfloat16),
+        match_down.astype(jnp.float32).astype(jnp.bfloat16),
+        gate,
+    )
+
+
+def expert_kernel(
+    chips, heads, experts, capacity, tile, group_size, all_ref, residual_ref, up_hbm, down_hbm, out_ref,
+    up_ref, down_ref, rows_ref, total_ref, gate_ref, back_ref, term_ref, got, outgoing, incoming,
+    weight_sem, pair_send, pair_recv, ring_send, ring_recv,
 ):
     ring = Ring(chips, heads)
     half = ring.count // 2
-    chunks = row_chunks(residual_ref.shape[0])
+    rows, width = residual_ref.shape
+    start = width % LANES
+    chunks = row_chunks(rows)
+    expert = lax.axis_index("ctx")
+    tiles = down_ref.shape[0] // tile
+
+    def loads(t):
+        span = pl.ds(pl.multiple_of(t * tile, 8), tile)
+        return [
+            pltpu.make_async_copy(up_hbm.at[0, span], up_ref.at[0, span], weight_sem.at[0, t]),
+            pltpu.make_async_copy(up_hbm.at[1, span], up_ref.at[1, span], weight_sem.at[1, t]),
+            pltpu.make_async_copy(down_hbm.at[span], down_ref.at[span], weight_sem.at[2, t]),
+        ]
+
+    for t in range(tiles):
+        for copy in loads(t):
+            copy.start()
     greet([ring.device(1), ring.device(-1), ring.partner])
+
     order = [half]
     for distance in range(half - 1, 0, -1):
         order += [distance, -distance]
     order.append(0)
-    shares = {}
-    for slot, offset in enumerate(order):
+    turned = (((1,), (1,)), ((), ()))
+
+    def block_of(index):
+        slot = lax.div(index, CORES)
+        distance = half - lax.div(slot + 1, 2)
+        sign = jnp.where(lax.rem(slot, 2) == 1, 1, -1)
+        return ring.block(sign * distance, lax.rem(index, CORES))
+
+    def compute(first, wait):
+        def collect(i, carry):
+            block = block_of(first + i)
+            tail = all_ref[block, :, width - start :]
+            place, back, gate = row_placement(tail, expert, experts, start, capacity)
+            span = pl.ds(pl.multiple_of(i * capacity, 16), capacity)
+            picked = jnp.dot(place, all_ref[block, :, :width], preferred_element_type=jnp.float32)
+            rows_ref[span, :] = picked.astype(jnp.bfloat16)
+            gate_ref[span, :] = gate
+            back_ref[i] = back
+            return carry
+
+        lax.fori_loop(0, group_size, collect, 0)
+
+        def multiply(t, carry):
+            if wait:
+                for copy in loads(t):
+                    copy.wait()
+            span = pl.ds(pl.multiple_of(t * tile, 8), tile)
+            x = rows_ref[...]
+            a = lax.dot_general(x, up_ref[0, span, :], turned, preferred_element_type=jnp.float32)
+            b = lax.dot_general(x, up_ref[1, span, :], turned, preferred_element_type=jnp.float32)
+            act = (a * jax.nn.sigmoid(1.702 * a) * (b + 1.0)).astype(jnp.bfloat16)
+            piece = jnp.dot(act, down_ref[span, :], preferred_element_type=jnp.float32)
+
+            @pl.when(t == 0)
+            def _():
+                total_ref[...] = piece
+
+            @pl.when(t > 0)
+            def _():
+                total_ref[...] = total_ref[...] + piece
+
+            return carry
+
+        lax.fori_loop(0, tiles, multiply, 0)
+
+        def spread(i, carry):
+            span = pl.ds(pl.multiple_of(i * capacity, 16), capacity)
+            gated = (total_ref[span, :] * gate_ref[span, :]).astype(jnp.bfloat16)
+            term = jnp.dot(back_ref[i], gated, preferred_element_type=jnp.float32)
+            term_ref[block_of(first + i)] = term.astype(jnp.bfloat16)
+            return carry
+
+        lax.fori_loop(0, group_size, spread, 0)
+
+    shares, arrived, hops = {}, set(), {}
+
+    def share(slot):
+        offset = order[slot]
         shares[offset] = remote(
             term_ref.at[ring.block(offset, 1 - ring.core)],
             got.at[slot],
@@ -339,7 +440,6 @@
             ring.partner,
         )
         shares[offset].start()
-    arrived = set()
 
     def pair(offset, chunk):
         if offset == -half:
@@ -350,8 +450,7 @@
         mine = term_ref[ring.block(offset, ring.core), chunk, :].astype(jnp.float32)
         return mine + got[order.index(offset), chunk, :].astype(jnp.float32)
 
-    hops = {}
-    for step in range(half):
+    def ring_step(step):
         for j, chunk in enumerate(chunks):
             for index, way in ((0, 1), (1, -1)):
                 if step == 0 and (j == 0) != (index == 0):
@@ -369,6 +468,16 @@
                     ring.device(way),
                 )
                 hops[index, step, j].start()
+
+    blocks, step = ring.count * CORES, 0
+    for first in range(0, blocks, group_size):
+        compute(first, first == 0)
+        done = (first + group_size) // CORES
+        for slot in range(first // CORES, done):
+            share(slot)
+        while step < half and 2 * step + 1 <= done:
+            ring_step(step)
+            step += 1
     for j, chunk in enumerate(chunks):
         total = pair(0, chunk) + residual_ref[chunk, :].astype(jnp.float32)
         for index in (0, 1):
@@ -380,34 +489,45 @@
         copy.wait_send()
 
 
-def sum_and_scatter(terms, residual):
+def experts_and_sum(gathered, residual, w_gate_up, w_down, experts, capacity):
     chips, heads = lax.axis_size("ctx") // CORES, lax.axis_size("head")
     rows, width = residual.shape
+    hidden = w_down.shape[1]
     half = chips * heads // 2
+    blocks = gathered.shape[0]
     parts = len(row_chunks(rows))
+    capacity = -(-capacity // 16) * 16
+    tile = hidden // 3 if hidden % 48 == 0 else hidden
+    group_size = blocks // 4
+    bf16, dma = jnp.bfloat16, pltpu.SemaphoreType.DMA
+    anywhere = pl.BlockSpec(memory_space=pl.ANY)
     return pl.pallas_call(
-        functools.partial(sum_kernel, chips, heads),
-        out_shape=jax.ShapeDtypeStruct((rows, width), jnp.bfloat16),
-        in_specs=[full_vmem()] * 2,
+        functools.partial(expert_kernel, chips, heads, experts, capacity, tile, group_size),
+        out_shape=jax.ShapeDtypeStruct((rows, width), bf16),
+        in_specs=[full_vmem(), full_vmem(), anywhere, anywhere],
         out_specs=full_vmem(),
         scratch_shapes=[
-            pltpu.VMEM((2 * half, rows, width), jnp.bfloat16),
-            pltpu.VMEM((2, half, rows, width), jnp.bfloat16),
-            pltpu.VMEM((2, half, rows, width), jnp.bfloat16),
-            pltpu.SemaphoreType.DMA((2 * half,)),
-            pltpu.SemaphoreType.DMA((2 * half,)),
-            pltpu.SemaphoreType.DMA((2, half, parts)),
-            pltpu.SemaphoreType.DMA((2, half, parts)),
+            pltpu.VMEM((2, hidden, width), bf16),
+            pltpu.VMEM((hidden, width), bf16),
+            pltpu.VMEM((group_size * capacity, width), bf16),
+            pltpu.VMEM((group_size * capacity, width), jnp.float32),
+            pltpu.VMEM((group_size * capacity, 1), jnp.float32),
+            pltpu.VMEM((group_size, rows, capacity), bf16),
+            pltpu.VMEM((blocks, rows, width), bf16),
+            pltpu.VMEM((2 * half, rows, width), bf16),
+            pltpu.VMEM((2, half, rows, width), bf16),
+            pltpu.VMEM((2, half, rows, width), bf16),
+            dma((3, hidden // tile)),
+            dma((2 * half,)),
+            dma((2 * half,)),
+            dma((2, half, parts)),
+            dma((2, half, parts)),
         ],
-        compiler_params=pltpu.CompilerParams(collective_id=2, has_side_effects=True),
-        name="sum_and_scatter",
-    )(terms, residual)
-
-
-def expert_activation(token_rows, w_gate_up):
-    gate_pre = jnp.dot(token_rows, w_gate_up[0, 0], preferred_element_type=jnp.float32)
-    up_pre = jnp.dot(token_rows, w_gate_up[0, 1], preferred_element_type=jnp.float32)
-    return (gate_pre * jax.nn.sigmoid(1.702 * gate_pre) * (up_pre + 1.0)).astype(jnp.bfloat16)
+        compiler_params=pltpu.CompilerParams(
+            collective_id=2, has_side_effects=True, vmem_limit_bytes=60 * 1024 * 1024
+        ),
+        name="experts_and_sum",
+    )(gathered, residual, jnp.swapaxes(w_gate_up[0], 1, 2), w_down[0])
 
 
 def body(
@@ -462,39 +582,7 @@
     own_hidden = lax.dynamic_slice_in_dim(hidden_in, row_start, own_rows, 0)
     own_routes = lax.dynamic_slice_in_dim(routes, row_start, own_rows, 0)
     residual, gathered = norm_and_gather(partial_sums, own_hidden, norm_gain, router, own_routes)
-    width, experts = router.shape
-    expert = lax.axis_index("ctx")
-    blocks = n_ctx * n_head
-    normed_all = gathered[:, :, :width]
-    lanes = jnp.arange(2 * experts, dtype=jnp.int32)
-    gate = jnp.sum(
-        jnp.where(
-            (lanes == expert) | (lanes == expert + experts),
-            gathered[:, :, width : width + 2 * experts].astype(jnp.float32),
-            0.0,
-        ),
-        axis=-1,
-    )
-    chosen = gate > 0.0
-    rank = jnp.cumsum(chosen.astype(jnp.int32), axis=1) - 1
-    place = (
-        (rank[:, None, :] == jnp.arange(capacity, dtype=jnp.int32)[None, :, None])
-        & chosen[:, None, :]
-    )
-    token_rows = jnp.einsum(
-        "bcr,brd->bcd",
-        place.astype(jnp.bfloat16),
-        normed_all,
-        preferred_element_type=jnp.float32,
-    ).astype(jnp.bfloat16)
-    row_gate = jnp.sum(jnp.where(place, gate[:, None, :], 0.0), axis=2).reshape(-1, 1)
-    activation = expert_activation(token_rows.reshape(blocks * capacity, -1), w_gate_up)
-    pieces = jnp.dot(activation, w_down[0], preferred_element_type=jnp.float32)
-    gated = (pieces * row_gate).astype(jnp.bfloat16).reshape(blocks, capacity, -1)
-    spread = jnp.einsum(
-        "bcr,bcd->brd", place.astype(jnp.bfloat16), gated, preferred_element_type=jnp.float32
-    ).astype(jnp.bfloat16)
-    return sum_and_scatter(spread, residual)
+    return experts_and_sum(gathered, residual, w_gate_up, w_down, router.shape[1], capacity)
 
 
 def solution(mesh):

time: 205 us -> 178 us (0.87)
  matrix products: 69.1 us -> 21.1 us
  Pallas kernels: 107 us -> 136 us
  local copies, waits for them, and re-layouts: 16.6 us -> 10.1 us
    dot_general x4 -> x0, matrix products: 48.1 us -> none  [the longest x1 24.8 us: body(): pieces = jnp.dot(activation, w_down[0], preferred_element_type=jnp.float32)]
    pallas_call x1, Pallas kernels: 39.1 us -> 68.7 us  [experts_and_sum(): pl.pallas_call(functools.partial(expert_kernel, chips, heads, experts, ca...]
    convert_element_type x1 -> x0, local copies, waits for them, and re-layouts: 6.49 us -> none  [body(): (pieces * row_gate).astype(jnp.bfloat16).reshape(blocks, capacity, -1)]
    unnamed x20 -> x16, local copies, waits for them, and re-layouts: 4.81 us -> 4.82 us
where the time goes in v3:
time: 178 us
  Pallas kernels  136 us (76%)
  matrix products  21.1 us (12%)
  local copies, waits for them, and re-layouts  10.1 us (6%)
  other arithmetic  10.1 us (6%)
    pallas_call x1, Pallas kernels, experts_and_sum(): pl.pallas_call(functools.partial(expert_kernel, chips, heads, experts, ca...  68.7 us
    pallas_call x1, Pallas kernels, norm_and_gather(): pl.pallas_call(functools.partial(norm_kernel, chips, heads, experts), out...  48.9 us
    pallas_call x1, Pallas kernels, gather_keys(): pl.pallas_call(functools.partial(line_kernel, chips), out_shape=(shape, s...  18.7 us
    reduce_sum x1, other arithmetic, fold_step(): running_sum = running_sum * rescale + jnp.sum(weights, axis=-1)  8.05 us
    dot_general x1, matrix products, fold_step(): jnp.einsum('cgtn,ncd->cgtd', weights.astype(jnp.bfloat16), value_grid, pr...  7.86 us
    dot_general x1, matrix products, fold_step(): jnp.einsum('tcgd,ncd->cgtn', query_grid, key_grid, preferred_element_type...  7.05 us
    dot_general x1, matrix products, body(): jnp.dot(attended, w_out, preferred_element_type=jnp.float32)  6.19 us
    unnamed x16, local copies, waits for them, and re-layouts  4.82 us

profile of v3, /device:TPU:0, one launch (start us, length us, event | category | flops | bytes accessed | tf_op | source)
XLA Modules:
  0.0 177.7 jit_solution(15769142799902359562)
XLA Ops:
  0.0 0.0 copy-start
  0.0 0.8 dynamic_slice.9
  0.9 0.9 fusion.17
  1.7 18.7 %gather_keys.1 = (bf16[8,128,256]{2,1,0:T(8,128)(2,1)}, bf16[8,128,256]{2,1,0:T(8,128)(2,1)}) custom-call(bf16[128,256]{1,0:T(8,128)(2,1)} %key_ref.1, bf16[128,256]{1,0:T(8,128)(2,1)} %value_ref.1), custom_call_target="tpu_custom_call" | custom-call | tf_op jit(solution)/shard_map/gather_keys/pallas_call | solution.py:184
  20.5 1.4 copy.27
  21.8 0.2 reshape.30
  22.1 1.3 copy.28
  23.4 0.0 copy-start.1
  23.4 7.0 %fusion = (f32[4,8,128]{2,1,0:T(8,128)S(1)}, f32[4,1024,128,8]{2,1,3,0:T(8,128)}) fusion(pred[128,1024]{0,1:T(8,128)(4,1)S(1)} %fusion.17, bf16[128,4,8,64]{0,3,2,1:T(8,128)(2,1)S(1)} %bitcast.51, bf16[1024,4,64,1]{0,2,1,3:T(8,128)(2,1)S(1)} %reshape.30), kind=kOutput, calls=%fused_computation.2 | convolution fusion | flops 549449728 | bytes 17973248 | tf_op jit(solution)/shard_map/tcgd,ncd->cgtn/dot_general | solution.py:23
  30.4 0.0 copy-done.5
  30.4 0.1 mul.27
  30.5 0.1 broadcast_maximum_fusion
  30.6 8.0 %fusion.1 = f32[4,8,128]{2,1,0:T(8,128)S(1)} fusion(f32[4,1024,128,8]{2,1,3,0:T(8,128)} %get-tuple-element.16, f32[4,8,128]{2,1,0:T(8,128)S(1)} %broadcast_maximum_fusion, pred[128,1024]{0,1:T(8,128)(4,1)S(1)} %fusion.17), kind=kLoop, calls=%fused_computation.3 | loop fusion | flops 20967424 | bytes 16941056 | tf_op jit(solution)/shard_map/reduce_sum | solution.py:32
  38.6 0.1 multiply_bitcast_fusion
  38.7 0.3 copy.29
  39.1 0.2 reshape.31
  39.3 7.9 %divide_convert_fusion = bf16[128,4,8,64]{0,3,2,1:T(8,128)(2,1)S(1)} fusion(f32[4,1024,128,8]{2,1,3,0:T(8,128)} %get-tuple-element.16, f32[4,8,128]{2,1,0:T(8,128)S(1)} %broadcast_maximum_fusion, pred[128,1024]{0,1:T(8,128)(4,1)S(1)} %fusion.17, bf16[1024,4,64,1]{0,2,1,3:T(8,128)(2,1)S(1)} %reshape.31, f32[128,4,8]{0,2,1:T(8,128)S(1)} %get-tuple-element.14, ...), kind=kOutput, calls=%fused_computation.10 | convolution fusion | flops 558628864 | bytes 18006016 | tf_op jit(solution)/shard_map/cgtn,ncd->cgtd/dot_general | solution.py:33
  47.2 0.0 copy-start.4
  47.2 0.0 copy-start.2
  47.2 0.0 copy-start.3
  47.2 6.2 %convolution_convert_fusion = bf16[128,2880]{0,1:T(8,128)(2,1)S(1)} fusion(bf16[2048,2880]{0,1:T(8,128)(2,1)} %param.19, bf16[128,2048]{0,1:T(8,128)(2,1)S(1)} %bitcast.53), kind=kOutput, calls=%fused_computation.7 | convolution fusion | flops 1510318080 | bytes 13058048 | tf_op jit(solution)/shard_map/dot_general | solution.py:581
  53.4 1.2 copy.33.part_ref
  54.6 0.3 constant_dynamic-slice_fusion.1
  54.9 1.0 copy.37.hidden_ref
  55.9 0.1 constant_dynamic-slice_fusion
  56.0 0.7 copy.38.route_ref
  56.7 0.1 pad.3.clone
  56.8 1.0 maximum_maximum_fusion.router_ref
  57.8 0.6 reshape.29.gain_ref
  58.4 48.9 %norm_and_gather.1 = (bf16[64,2880]{1,0:T(8,128)(2,1)}, bf16[16,64,2944]{2,1,0:T(8,128)(2,1)}) custom-call(bf16[128,2880]{1,0:T(8,128)(2,1)} %copy.33.part_ref, bf16[64,2880]{1,0:T(8,128)(2,1)} %copy.37.hidden_ref, f32[1,2880]{1,0:T(1,128)} %reshape.29.gain_ref, bf16[128,2880]{1,0:T(8,128)(2,1)} %maximum_maximum_fusion.router_ref, s32[64,4]{1,0:T(8,128)} %copy.38.route_ref), custom_call_target="tpu_custom_call" | custom-call | tf_op jit(solution)/shard_map/norm_and_gather/pallas_call | solution.py:298
  107.3 68.7 %experts_and_sum.1 = bf16[64,2880]{1,0:T(8,128)(2,1)} custom-call(bf16[16,64,2944]{2,1,0:T(8,128)(2,1)} %get-tuple-element.11.all_ref, bf16[64,2880]{1,0:T(8,128)(2,1)} %get-tuple-element.12.residual_ref, bf16[2,1440,2880]{2,1,0:T(8,128)(2,1)} %bitcast.49, bf16[1440,2880]{1,0:T(8,128)(2,1)} %bitcast.50), custom_call_target="tpu_custom_call" | custom-call | tf_op jit(solution)/shard_map/experts_and_sum/pallas_call | solution.py:504
  176.0 1.8 copy.40
  (10 shorter events, 0.0 us)
Async XLA Ops:
  0.0 54.6 %copy-start = (bf16[128,2880]{0,1:T(8,128)(2,1)S(1)}, bf16[128,2880]{0,1:T(8,128)(2,1)}, u32[]{:S(2)}) copy-start(bf16[128,2880]{0,1:T(8,128)(2,1)} %param.17) | copy-start | bytes 2211844
  0.0 30.4 %copy-start.5 = (f32[32]{0:T(128)S(1)}, f32[32]{0:T(128)}, u32[]{:S(2)}) copy-start(f32[32]{0:T(128)} %param.15) | copy-start | bytes 388
  23.4 15.4 %copy-start.1 = (bf16[8,128,256]{2,1,0:T(8,128)(2,1)S(1)}, bf16[8,128,256]{2,1,0:T(8,128)(2,1)}, u32[]{:S(2)}) copy-start(bf16[8,128,256]{2,1,0:T(8,128)(2,1)} %get-tuple-element.10) | copy-start | bytes 1572868
  47.2 8.7 %copy-start.4 = (s32[128,4]{0,1:T(4,128)S(1)}, s32[128,4]{0,1:T(4,128)}, u32[]{:S(2)}) copy-start(s32[128,4]{0,1:T(4,128)} %param.18) | copy-start | bytes 6148
  47.2 9.6 %copy-start.2 = (bf16[2880,8]{0,1:T(8,128)(2,1)S(1)}, bf16[2880,8]{0,1:T(8,128)(2,1)}, u32[]{:S(2)}) copy-start(bf16[2880,8]{0,1:T(8,128)(2,1)} %param.21) | copy-start | bytes 138244
  47.2 10.6 %copy-start.3 = (f32[2880]{0:T(1024)S(1)}, f32[2880]{0:T(1024)}, u32[]{:S(2)}) copy-start(f32[2880]{0:T(1024)} %param.20) | copy-start | bytes 34564

commit v4 on v3

--- a/solution.py
+++ b/solution.py
@@ -13,30 +13,54 @@
 masked_value = -1e30
 
 
-def fold_step(state_in, pieces, query_grid, tok_pos, tok_seg, segments):
-    running_max, running_sum, weighted = state_in
-    key_piece, value_piece = pieces
-    row_count = key_piece.shape[0]
-    kv_groups = query_grid.shape[1]
-    key_grid = key_piece.reshape(row_count, kv_groups, -1)
-    value_grid = value_piece.reshape(row_count, kv_groups, -1)
-    scores = jnp.einsum(
-        "tcgd,ncd->cgtn", query_grid, key_grid, preferred_element_type=jnp.float32
-    ) * HEAD_SIZE ** (-0.5)
-    key_pos = jnp.arange(row_count, dtype=jnp.int32)
-    visible = (key_pos[None, :] <= tok_pos[:, None]) & (segments[None, :] == tok_seg[:, None])
-    scores = jnp.where(visible, scores, masked_value)
-    new_max = jnp.maximum(running_max, jnp.max(scores, axis=-1))
-    weights = jnp.where(visible, jnp.exp(scores - new_max[..., None]), 0.0)
-    rescale = jnp.exp(running_max - new_max)
-    running_sum = running_sum * rescale + jnp.sum(weights, axis=-1)
-    weighted = weighted * rescale[..., None] + jnp.einsum(
-        "cgtn,ncd->cgtd",
-        weights.astype(jnp.bfloat16),
-        value_grid,
-        preferred_element_type=jnp.float32,
+def attend_kernel(
+    query_ref, key_ref, value_ref, sink_ref, place_ref, segment_ref, own_segment_ref, out_ref
+):
+    rows = query_ref.shape[0]
+    kv_groups = key_ref.shape[1] // HEAD_SIZE
+    share = query_ref.shape[1] // key_ref.shape[1]
+    spot = lax.broadcasted_iota(jnp.int32, (rows, key_ref.shape[0]), 1)
+    visible = (spot <= place_ref[...]) & (segment_ref[...] == own_segment_ref[...])
+    hidden_bias = jnp.where(visible, 0.0, masked_value)
+    for group in range(kv_groups):
+        span = slice(group * HEAD_SIZE, (group + 1) * HEAD_SIZE)
+        group_keys = key_ref[:, span]
+        group_values = value_ref[:, span]
+        for pair in range(share // 2):
+            both = []
+            for member in range(2):
+                head = group * share + pair * 2 + member
+                query = query_ref[:, head * HEAD_SIZE : (head + 1) * HEAD_SIZE]
+                scores = lax.dot_general(
+                    query, group_keys, (((1,), (1,)), ((), ())), preferred_element_type=jnp.float32
+                )
+                scores = scores * HEAD_SIZE ** (-0.5) + hidden_bias
+                sink = sink_ref[:, head : head + 1]
+                top = jnp.maximum(jnp.max(scores, axis=-1, keepdims=True), sink)
+                weights = jnp.exp(scores - top)
+                total = jnp.sum(weights, axis=-1, keepdims=True) + jnp.exp(sink - top)
+                mixed = jnp.dot(weights.astype(jnp.bfloat16), group_values, preferred_element_type=jnp.float32)
+                both.append((mixed / total).astype(jnp.bfloat16))
+            first = (group * share + pair * 2) * HEAD_SIZE
+            out_ref[:, first : first + 2 * HEAD_SIZE] = jnp.concatenate(both, axis=1)
+
+
+def attend(queries, all_keys, all_values, sinks, tok_pos, tok_seg, segments):
+    return pl.pallas_call(
+        attend_kernel,
+        out_shape=jax.ShapeDtypeStruct(queries.shape, jnp.bfloat16),
+        in_specs=[full_vmem()] * 7,
+        out_specs=full_vmem(),
+        name="attend",
+    )(
+        queries,
+        all_keys,
+        all_values,
+        sinks.reshape(1, -1),
+        tok_pos.reshape(-1, 1),
+        segments.reshape(1, -1),
+        tok_seg.reshape(-1, 1),
     )
-    return (new_max, running_sum, weighted)
 
 
 MESH = pl.DeviceIdType.MESH
@@ -548,33 +572,11 @@
     n_head = lax.axis_size("head")
     tok_count = queries.shape[0]
     top_count = routes.shape[1]
-    kv_groups = keys.shape[1] // HEAD_SIZE
-    group_share = queries.shape[1] // (kv_groups * HEAD_SIZE)
     q_start = lax.axis_index("ctx") * tok_count
     tok_pos = q_start + jnp.arange(tok_count, dtype=jnp.int32)
     tok_seg = lax.dynamic_slice_in_dim(segments, q_start, tok_count, 0)
-    query_grid = queries.reshape(tok_count, kv_groups, group_share, HEAD_SIZE)
-    sink_grid = sinks.reshape(kv_groups, group_share, 1) * jnp.ones((1, 1, tok_count), jnp.float32)
-    initial = (
-        sink_grid,
-        jnp.ones_like(sink_grid),
-        jnp.zeros((kv_groups, group_share, tok_count, HEAD_SIZE), jnp.float32),
-    )
     all_keys, all_values = gather_keys(keys, values)
-    running_max, running_sum, weighted = fold_step(
-        initial,
-        (all_keys, all_values),
-        query_grid,
-        tok_pos,
-        tok_seg,
-        segments,
-    )
-    attended = (
-        (weighted / running_sum[..., None])
-        .transpose(2, 0, 1, 3)
-        .reshape(tok_count, -1)
-        .astype(jnp.bfloat16)
-    )
+    attended = attend(queries, all_keys, all_values, sinks, tok_pos, tok_seg, segments)
     own_rows = tok_count // n_head
     row_start = lax.axis_index("head") * own_rows
     capacity = max(2, min(tok_count // n_head, 3 * tok_count * top_count // (2 * n_head * n_ctx)))

time: 178 us -> 173 us (0.972)
  Pallas kernels: 136 us -> 155 us
  matrix products: 21.1 us -> 7.95 us
  other arithmetic: 10.1 us -> 1.65 us
    pallas_call x0 -> x1, Pallas kernels: none -> 18.3 us  [attend(): pl.pallas_call(attend_kernel, out_shape=jax.ShapeDtypeStruct(queries.shap...]
    dot_general x2 -> x0, matrix products: 14.9 us -> none  [the longest x1 7.86 us: fold_step(): jnp.einsum('cgtn,ncd->cgtd', weights.astype(jnp.bfloat16), value_grid, pr...]
    reduce_sum x1 -> x0, other arithmetic: 8.05 us -> none  [fold_step(): running_sum = running_sum * rescale + jnp.sum(weights, axis=-1)]
    unnamed x16 -> x7, local copies, waits for them, and re-layouts: 4.82 us -> 3.48 us
where the time goes in v4:
time: 173 us
  Pallas kernels  155 us (90%)
  local copies, waits for them, and re-layouts  8.62 us (5%)
  matrix products  7.95 us (5%)
    pallas_call x1, Pallas kernels, experts_and_sum(): pl.pallas_call(functools.partial(expert_kernel, chips, heads, experts, ca...  68.8 us
    pallas_call x1, Pallas kernels, norm_and_gather(): pl.pallas_call(functools.partial(norm_kernel, chips, heads, experts), out...  48.9 us
    pallas_call x1, Pallas kernels, gather_keys(): pl.pallas_call(functools.partial(line_kernel, chips), out_shape=(shape, s...  18.6 us
    pallas_call x1, Pallas kernels, attend(): pl.pallas_call(attend_kernel, out_shape=jax.ShapeDtypeStruct(queries.shap...  18.3 us
    dot_general x1, matrix products, body(): jnp.dot(attended, w_out, preferred_element_type=jnp.float32)  7.95 us
    unnamed x7, local copies, waits for them, and re-layouts  3.48 us

profile of v4, /device:TPU:0, one launch (start us, length us, event | category | flops | bytes accessed | tf_op | source)
XLA Modules:
  0.0 172.9 jit_solution(10834967979748716670)
XLA Ops:
  0.0 0.0 copy-start
  0.0 0.0 copy-start.1
  0.0 0.8 dynamic-slice_bitcast_fusion
  0.8 0.1 pad.3.clone
  0.9 0.8 constant_dynamic-slice_fusion
  1.7 1.3 reshape.31.gain_ref
  3.0 0.7 copy.22.route_ref
  3.7 0.7 copy.17.own_segment_ref
  4.4 0.6 iota_add_fusion.place_ref
  5.1 0.0 copy-done
  5.1 0.3 constant_dynamic-slice_fusion.1
  5.3 1.0 copy.21.hidden_ref
  6.3 0.0 copy-done.1
  6.3 1.0 maximum_maximum_fusion.router_ref
  7.4 18.6 %gather_keys.1 = (bf16[8,128,256]{2,1,0:T(8,128)(2,1)}, bf16[8,128,256]{2,1,0:T(8,128)(2,1)}) custom-call(bf16[128,256]{1,0:T(8,128)(2,1)} %key_ref.1, bf16[128,256]{1,0:T(8,128)(2,1)} %value_ref.1), custom_call_target="tpu_custom_call" | custom-call | tf_op jit(solution)/shard_map/gather_keys/pallas_call | solution.py:208
  26.0 18.3 %attend.1 = bf16[128,2048]{1,0:T(8,128)(2,1)} custom-call(bf16[128,2048]{1,0:T(8,128)(2,1)} %query_ref.1, bf16[1024,256]{1,0:T(8,128)(2,1)} %bitcast.15, bf16[1024,256]{1,0:T(8,128)(2,1)} %bitcast.16, f32[1,32]{1,0:T(1,128)} %bitcast.19, s32[128,1]{1,0:T(8,128)} %iota_add_fusion.place_ref, s32[1,1024]{1,0:T(1,128)} %bitcast.18, s32[128,1]{1,0:T(8,128)} %copy.17.own_segment_ref), custom_call_target="tpu_custom_call" | custom-call | tf_op jit(solution)/shard_map/attend/pallas_call | solution.py:49
  44.3 7.9 %convolution_convert_fusion = bf16[128,2880]{0,1:T(8,128)(2,1)S(1)} fusion(bf16[128,2048]{1,0:T(8,128)(2,1)} %attend.1, bf16[2048,2880]{0,1:T(8,128)(2,1)} %param.19), kind=kOutput, calls=%fused_computation | convolution fusion | flops 1510318080 | bytes 13058048 | tf_op jit(solution)/shard_map/dot_general | solution.py:583
  52.2 1.2 copy.20.part_ref
  53.4 48.9 %norm_and_gather.1 = (bf16[64,2880]{1,0:T(8,128)(2,1)}, bf16[16,64,2944]{2,1,0:T(8,128)(2,1)}) custom-call(bf16[128,2880]{1,0:T(8,128)(2,1)} %copy.20.part_ref, bf16[64,2880]{1,0:T(8,128)(2,1)} %copy.21.hidden_ref, f32[1,2880]{1,0:T(1,128)} %reshape.31.gain_ref, bf16[128,2880]{1,0:T(8,128)(2,1)} %maximum_maximum_fusion.router_ref, s32[64,4]{1,0:T(8,128)} %copy.22.route_ref), custom_call_target="tpu_custom_call" | custom-call | tf_op jit(solution)/shard_map/norm_and_gather/pallas_call | solution.py:322
  102.3 68.8 %experts_and_sum.1 = bf16[64,2880]{1,0:T(8,128)(2,1)} custom-call(bf16[16,64,2944]{2,1,0:T(8,128)(2,1)} %get-tuple-element.11.all_ref, bf16[64,2880]{1,0:T(8,128)(2,1)} %get-tuple-element.12.residual_ref, bf16[2,1440,2880]{2,1,0:T(8,128)(2,1)} %bitcast.13, bf16[1440,2880]{1,0:T(8,128)(2,1)} %bitcast.14), custom_call_target="tpu_custom_call" | custom-call | tf_op jit(solution)/shard_map/experts_and_sum/pallas_call | solution.py:528
  171.2 1.8 %copy.24 = bf16[64,2880]{1,0:T(8,128)(2,1)} copy(bf16[64,2880]{1,0:T(8,128)(2,1)} %experts_and_sum.1) | data formatting | bytes 737280
  (3 shorter events, 0.0 us)
Async XLA Ops:
  0.0 5.1 %copy-start = (bf16[128,2880]{0,1:T(8,128)(2,1)S(1)}, bf16[128,2880]{0,1:T(8,128)(2,1)}, u32[]{:S(2)}) copy-start(bf16[128,2880]{0,1:T(8,128)(2,1)} %param.17) | copy-start | bytes 2211844
  0.0 6.3 %copy-start.1 = (bf16[2880,8]{0,1:T(8,128)(2,1)S(1)}, bf16[2880,8]{0,1:T(8,128)(2,1)}, u32[]{:S(2)}) copy-start(bf16[2880,8]{0,1:T(8,128)(2,1)} %param.21) | copy-start | bytes 138244
